TPU v7x, 32 devices: a whole 2x2x4 slice. The times are simulated.
32 devices in a mesh: dp: 8 (over z, x), mp: 4 (over y, core).
Axes of the slice: x: 2, y: 2, z: 4, core: 2. Of those that a mesh axis runs over, the one named last changes fastest.
Arguments:
- block_input: bfloat16 [16384, 768], P('dp'), may hold values from -6 to 6
- segment_ids: int32 [16, 1024], P('dp'), may hold values from 0 to 7, never falling along the last dimension, each value on 1 to 256 neighbouring positions
- group_ids: int32 [16, 1024], P('dp'), may hold values from 0 to 3
- padding: int32 [16, 1024], P('dp'), may hold values 0 or 1
- ln1_gain: float32 [768], replicated, may hold values from 0.25 to 1.75
- ln1_bias: float32 [768], replicated, may hold values from -4 to 4
- w_qkv: bfloat16 [768, 3, 768], P(None, None, 'mp'), may hold values from -0.21875 to 0.21875
- b_qv: float32 [2, 768], P(None, 'mp'), may hold values from -1.5 to 1.5
- w_out: bfloat16 [768, 768], P('mp'), may hold values from -1.75 to 1.75
- b_out: float32 [768], replicated, may hold values from -4 to 4
- ln2_gain: float32 [768], replicated, may hold values from 0.25 to 1.75
- ln2_bias: float32 [768], replicated, may hold values from -4 to 4
- w_up: bfloat16 [768, 3072], P(None, 'mp'), may hold values from -0.21875 to 0.21875
- b_up: float32 [3072], P('mp'), may hold values from -6 to 6
- w_down: bfloat16 [3072, 768], P('mp'), may hold values from -0.15625 to 0.15625
- b_down: float32 [768], replicated, may hold values from -4 to 4
- cotangent: bfloat16 [16384, 768], P('dp'), may hold values from -6 to 6
Outputs:
- block_output: bfloat16 [16384, 768], P('dp')
- input_grad: float32 [16384, 768], P('dp')
- grad_ln1_gain: float32 [768], P('dp')
- grad_ln1_bias: float32 [768], P('dp')
- grad_w_qkv: float32 [768, 3, 768], P('dp', None, 'mp')
- grad_b_qv: float32 [2, 768], P(None, ('mp', 'dp'))
- grad_w_out: float32 [768, 768], P('mp', 'dp')
- grad_b_out: float32 [768], P('dp')
- grad_ln2_gain: float32 [768], P('dp')
- grad_ln2_bias: float32 [768], P('dp')
- grad_w_up: float32 [768, 3072], P('dp', 'mp')
- grad_b_up: float32 [3072], P(('mp', 'dp'))
- grad_w_down: float32 [3072, 768], P('mp', 'dp')
- grad_b_down: float32 [768], P('dp')
Inputs may be any that keep to these rules, and one draw needn't show every extreme that they name: `segment_ids`: along each sequence the segment numbers never fall; a segment holds at most 256 tokens.
All inputs are finite; a program needn't handle non-finite values. No bound on the sum of `padding` on one device may be relied on, other than what follows from the above.
Results may differ from a plain program's by a relative error of at most 0.018.
Values may be sent and summed in bfloat16 or wider, within the bound.
No kernel may reach another device: no remote copies, remote signals or barrier semaphores. Data moves between devices by JAX's collectives and lax.ppermute only.
A program may use at most 128 MiB of HBM per device.

v0:
```python
import jax
import jax.numpy as jnp
from jax import lax
from jax.sharding import PartitionSpec as P

HD = 64


def layer_norm(values):
    average = jnp.mean(values, -1, keepdims=True)
    centered = values - average
    variance = jnp.mean(centered * centered, -1, keepdims=True)
    return centered * lax.rsqrt(variance + 1e-05)


def norm_apply(values, norm_gain, norm_bias):
    return layer_norm(values) * norm_gain + norm_bias


def norm_grads(values, norm_gain, norm_bias, upstream):
    unused_out, back_fn = jax.vjp(norm_apply, values, norm_gain, norm_bias)
    return back_fn(upstream)


def exact_gelu(values):
    return jax.nn.gelu(values, approximate=False)


def make_allowed(segment_row, group_row, padding_row):
    position = jnp.arange(segment_row.shape[0])
    same_segment = segment_row[:, None] == segment_row[None, :]
    earlier = group_row[None, :] <= group_row[:, None]
    visible = padding_row[None, :] == 0
    return same_segment & earlier & visible | (position[:, None] == position[None, :])


def masked_scores(queries, key_rows, segment_row, group_row, padding_row):
    allowed = make_allowed(segment_row, group_row, padding_row)
    scores = (
        jnp.einsum("qhd,khd->hqk", queries, key_rows, preferred_element_type=jnp.float32) * 0.125
    )
    return jnp.where(allowed[None], scores, -1e30)


def attend_forward(operands):
    queries, key_rows, value_rows, segment_row, group_row, padding_row = operands
    scores = masked_scores(queries, key_rows, segment_row, group_row, padding_row)
    highest = jnp.max(scores, -1, keepdims=True)
    weights = jnp.exp(scores - highest)
    total = jnp.sum(weights, -1, keepdims=True)
    softmax_out = weights / total
    log_total = highest[..., 0] + jnp.log(total[..., 0])
    context = jnp.einsum(
        "hqk,khd->qhd",
        softmax_out.astype(jnp.bfloat16),
        value_rows,
        preferred_element_type=jnp.float32,
    )
    return (context.astype(jnp.bfloat16), log_total)


def attend_backward(operands):
    queries, key_rows, value_rows, segment_row, group_row, padding_row, log_total, context_grad = (
        operands
    )
    scores = masked_scores(queries, key_rows, segment_row, group_row, padding_row)
    softmax_out = jnp.exp(scores - log_total[:, :, None])
    value_grad = jnp.einsum(
        "hqk,qhd->khd",
        softmax_out.astype(jnp.bfloat16),
        context_grad,
        preferred_element_type=jnp.float32,
    )
    prob_grad = jnp.einsum(
        "qhd,khd->hqk", context_grad, value_rows, preferred_element_type=jnp.float32
    )
    score_grad = softmax_out * (prob_grad - jnp.sum(softmax_out * prob_grad, -1, keepdims=True))
    score_grad = score_grad.astype(jnp.bfloat16)
    query_grad = (
        jnp.einsum("hqk,khd->qhd", score_grad, key_rows, preferred_element_type=jnp.float32) * 0.125
    )
    key_grad = (
        jnp.einsum("hqk,qhd->khd", score_grad, queries, preferred_element_type=jnp.float32) * 0.125
    )
    return (
        query_grad.astype(jnp.bfloat16),
        key_grad.astype(jnp.bfloat16),
        value_grad.astype(jnp.bfloat16),
    )


def body(
    block_input,
    segment_ids,
    group_ids,
    padding,
    ln1_gain,
    ln1_bias,
    w_qkv,
    b_qv,
    w_out,
    b_out,
    ln2_gain,
    ln2_bias,
    w_up,
    b_up,
    w_down,
    b_down,
    cotangent,
):
    stream = block_input.astype(jnp.float32)
    sequences, length = segment_ids.shape
    row_count = stream.shape[0]
    local_width = w_qkv.shape[2]
    local_heads = local_width // HD
    block_shape = (sequences, length, local_heads, HD)
    normed_one = norm_apply(stream, ln1_gain, ln1_bias).astype(jnp.bfloat16)
    projected = jnp.einsum("td,dje->tje", normed_one, w_qkv, preferred_element_type=jnp.float32)
    queries = (projected[:, 0] + b_qv[0]).astype(jnp.bfloat16).reshape(block_shape)
    key_rows = projected[:, 1].astype(jnp.bfloat16).reshape(block_shape)
    value_rows = (projected[:, 2] + b_qv[1]).astype(jnp.bfloat16).reshape(block_shape)
    context, log_total = lax.map(
        attend_forward, (queries, key_rows, value_rows, segment_ids, group_ids, padding)
    )
    context = context.reshape(row_count, local_width)
    attn_part = jnp.dot(context, w_out, preferred_element_type=jnp.float32)
    attn_out = lax.psum(attn_part.astype(jnp.bfloat16), "mp").astype(jnp.float32) + b_out
    residual = stream + attn_out
    normed_two = norm_apply(residual, ln2_gain, ln2_bias).astype(jnp.bfloat16)
    up_proj = jnp.dot(normed_two, w_up, preferred_element_type=jnp.float32) + b_up
    activated, gelu_back = jax.vjp(exact_gelu, up_proj)
    hidden = activated.astype(jnp.bfloat16)
    mlp_part = jnp.dot(hidden, w_down, preferred_element_type=jnp.float32)
    mlp_out = lax.psum(mlp_part.astype(jnp.bfloat16), "mp").astype(jnp.float32) + b_down
    block_output = (residual + mlp_out).astype(jnp.bfloat16)
    out_grad = cotangent.astype(jnp.float32)
    grad_b_down = jnp.sum(out_grad, 0)
    grad_w_down = jnp.einsum("tf,td->fd", hidden, cotangent, preferred_element_type=jnp.float32)
    hidden_grad = jnp.einsum("td,fd->tf", cotangent, w_down, preferred_element_type=jnp.float32)
    up_grad = gelu_back(hidden_grad)[0].astype(jnp.bfloat16)
    grad_b_up = jnp.sum(up_grad.astype(jnp.float32), 0)
    grad_w_up = jnp.einsum("td,tf->df", normed_two, up_grad, preferred_element_type=jnp.float32)
    normed_two_grad = jnp.einsum("tf,df->td", up_grad, w_up, preferred_element_type=jnp.float32)
    summed_grad = lax.psum(normed_two_grad.astype(jnp.bfloat16), "mp").astype(jnp.float32)
    back_full, grad_ln2_gain, grad_ln2_bias = norm_grads(residual, ln2_gain, ln2_bias, summed_grad)
    residual_grad = out_grad + back_full
    grad_b_out = jnp.sum(residual_grad, 0)
    attn_grad = residual_grad.astype(jnp.bfloat16)
    grad_w_out = jnp.einsum("tc,td->cd", context, attn_grad, preferred_element_type=jnp.float32)
    context_grad = jnp.einsum(
        "td,cd->tc", attn_grad, w_out, preferred_element_type=jnp.float32
    ).astype(jnp.bfloat16)
    query_grad, key_grad, value_grad = lax.map(
        attend_backward,
        (
            queries,
            key_rows,
            value_rows,
            segment_ids,
            group_ids,
            padding,
            log_total,
            context_grad.reshape(block_shape),
        ),
    )
    query_grad = query_grad.reshape(row_count, local_width)
    key_grad = key_grad.reshape(row_count, local_width)
    value_grad = value_grad.reshape(row_count, local_width)
    proj_grad = jnp.stack([query_grad, key_grad, value_grad], axis=1)
    grad_b_qv = jnp.stack(
        [jnp.sum(query_grad.astype(jnp.float32), 0), jnp.sum(value_grad.astype(jnp.float32), 0)]
    )
    grad_w_qkv = jnp.einsum(
        "td,tje->dje", normed_one, proj_grad, preferred_element_type=jnp.float32
    )
    normed_one_grad = jnp.einsum(
        "tje,dje->td", proj_grad, w_qkv, preferred_element_type=jnp.float32
    )
    summed_one = lax.psum(normed_one_grad.astype(jnp.bfloat16), "mp").astype(jnp.float32)
    back_one, grad_ln1_gain, grad_ln1_bias = norm_grads(stream, ln1_gain, ln1_bias, summed_one)
    input_grad = residual_grad + back_one
    shards = (
        lax.psum_scatter(grad_ln1_gain, "dp", scatter_dimension=0, tiled=True),
        lax.psum_scatter(grad_ln1_bias, "dp", scatter_dimension=0, tiled=True),
        lax.psum_scatter(grad_w_qkv, "dp", scatter_dimension=0, tiled=True),
        lax.psum_scatter(grad_b_qv, "dp", scatter_dimension=1, tiled=True),
        lax.psum_scatter(grad_w_out, "dp", scatter_dimension=1, tiled=True),
        lax.psum_scatter(grad_b_out, "dp", scatter_dimension=0, tiled=True),
        lax.psum_scatter(grad_ln2_gain, "dp", scatter_dimension=0, tiled=True),
        lax.psum_scatter(grad_ln2_bias, "dp", scatter_dimension=0, tiled=True),
        lax.psum_scatter(grad_w_up, "dp", scatter_dimension=0, tiled=True),
        lax.psum_scatter(grad_b_up, "dp", scatter_dimension=0, tiled=True),
        lax.psum_scatter(grad_w_down, "dp", scatter_dimension=1, tiled=True),
        lax.psum_scatter(grad_b_down, "dp", scatter_dimension=0, tiled=True),
    )
    return (
        block_output,
        input_grad,
        shards[0],
        shards[1],
        shards[2],
        shards[3],
        shards[4],
        shards[5],
        shards[6],
        shards[7],
        shards[8],
        shards[9],
        shards[10],
        shards[11],
    )


def solution(mesh):
    return jax.shard_map(
        body,
        mesh=mesh,
        in_specs=(
            P("dp", None),
            P("dp", None),
            P("dp", None),
            P("dp", None),
            P(),
            P(),
            P(None, None, "mp"),
            P(None, "mp"),
            P("mp", None),
            P(),
            P(),
            P(),
            P(None, "mp"),
            P("mp"),
            P("mp", None),
            P(),
            P("dp", None),
        ),
        out_specs=(
            P("dp", None),
            P("dp", None),
            P("dp"),
            P("dp"),
            P("dp", None, "mp"),
            P(None, ("mp", "dp")),
            P("mp", "dp"),
            P("dp"),
            P("dp"),
            P("dp"),
            P("dp", "mp"),
            P(("mp", "dp")),
            P("mp", "dp"),
            P("dp"),
        ),
        check_vma=False,
    )
```

profile of v0, /device:TPU:0, one launch (start us, length us, event | category | flops | bytes accessed | tf_op | source)
XLA Modules:
  0.0 709.1 jit_solution(16245805525987791740)
XLA Ops:
  7.3 2.5 convert_reduce_fusion.2
  9.8 2.9 fusion.72
  13.4 2.3 fusion.101
  18.6 3.6 squeeze.39
  22.2 1.4 convert_element_type.112
  25.0 2.5 squeeze.38
  27.5 2.9 fusion.87
  31.4 48.8 %while.26 = (s32[]{:T(128)}, bf16[2,1024,3,64]{1,3,2,0:T(8,128)(2,1)}, f32[2,3,1024]{2,1,0:T(4,128)}, bf16[2,1024,3,64]{1,3,2,0:T(8,128)(2,1)S(1)}, s32[2,1024]{...) while((s32[]{:T(128)}, ...), condition=%wide.region_5.6_spmd, body=%wide.region_2.5_spmd.sunk | while | flops 849541120 | bytes 50155752 | solution.py:122
  32.1 1.8 fusion.148
  33.9 5.9 fusion.149
  39.9 7.4 %fusion.150 = f32[3,1024]{1,0:T(4,128)S(1)} fusion(f32[3,1024,1024]{1,2,0:T(8,128)} %get-tuple-element.402, f32[3,1024]{1,0:T(4,128)S(1)} %get-tuple-element.403, pred[1024,1024]{0,1:T(8,128)(4,1)S(1)} %fusion.148), kind=kLoop, calls=%fused_computation.4.clone.1 | loop fusion | flops 12579840 | bytes 13656064 | tf_op jit(solution)/shard_map/while/body/eval_jaxpr/reduce_sum | solution.py:50
  47.3 6.8 fusion.151
  56.4 1.8 fusion.148
  58.2 5.9 fusion.149
  64.1 7.4 %fusion.150 = f32[3,1024]{1,0:T(4,128)S(1)} fusion(f32[3,1024,1024]{1,2,0:T(8,128)} %get-tuple-element.402, f32[3,1024]{1,0:T(4,128)S(1)} %get-tuple-element.403, pred[1024,1024]{0,1:T(8,128)(4,1)S(1)} %fusion.148), kind=kLoop, calls=%fused_computation.4.clone.1 | loop fusion | flops 12579840 | bytes 13656064 | tf_op jit(solution)/shard_map/while/body/eval_jaxpr/reduce_sum | solution.py:50
  71.5 6.8 fusion.151
  80.1 2.2 copy.65
  82.6 3.7 convolution_convert_fusion.2
  86.3 71.2 %all-reduce.14.cloned.1.call-done = bf16[2048,768]{1,0:T(8,128)(2,1)} async-done(((bf16[2048,768]{1,0:T(8,128)(2,1)}), bf16[2048,768]{1,0:T(8,128)(2,1)}) %all-reduce.14.cloned.1.call-update) | async-done | bytes 3145744 | tf_op jit(solution)/shard_map/psum | solution.py:127
  157.6 4.1 fusion.83
  162.3 2.4 multiply_reduce_fusion.1
  165.4 4.7 fusion.99
  170.1 19.1 %convert_reduce_fusion.4 = (f32[768]{0:T(1024)}, bf16[2048,768]{1,0:T(8,128)(2,1)S(1)}, f32[2048,768]{1,0:T(8,128)}) fusion(f32[2048,768]{1,0:T(8,128)S(1)} %fusion.99, f32[768]{0:T(1024)S(1)} %copy-done.58, bf16[2048,768]{1,0:T(8,128)(2,1)S(1)} %copy-done.24, bf16[768,768]{1,0:T(8,128)(2,1)S(1)} %copy-done), kind=kOutput, calls=%fused_computation.103 | convolution fusion | flops 2533883136 | bytes 20060160 | tf_op jit(solution)/shard_map/td,fd->tf/dot_general | solution.py:139
  189.2 1.7 copy-done.68
  190.9 4.0 convolution_convert_fusion
  195.0 5.5 multiply_convert_fusion.1
  200.5 1.8 copy-done.23
  202.2 4.5 convolution_convert_fusion.1
  206.7 56.9 %all-reduce.16.cloned.1.call-done = bf16[2048,768]{1,0:T(8,128)(2,1)} async-done(((bf16[2048,768]{1,0:T(8,128)(2,1)}), bf16[2048,768]{1,0:T(8,128)(2,1)}) %all-reduce.16.cloned.1.call-update) | async-done | bytes 3145744 | tf_op jit(solution)/shard_map/psum | solution.py:144
  263.6 5.9 convert_reduce_fusion.1
  270.2 5.2 fusion.75
  275.4 4.6 fusion.106
  280.0 2.7 copy-done.7
  282.7 2.3 fusion.92
  285.0 4.0 convolution_convert_fusion.3
  289.1 1.4 reshape.332
  294.8 52.4 %while.27 = (s32[]{:T(128)}, bf16[2,1024,3,64]{1,3,2,0:T(8,128)(2,1)}, bf16[2,1024,3,64]{1,3,2,0:T(8,128)(2,1)}, bf16[2,1024,3,64]{1,3,2,0:T(8,128)(2,1)}, bf16[...) while((s32[]{:T(128)}, ...), condition=%wide.region_15.16_spmd, body=%wide.region_13.15_spmd.sunk | while | flops 2067724288 | bytes 124648808 | solution.py:153
  295.1 1.8 fusion.161
  296.9 1.8 fusion.160
  298.8 3.7 fusion.164
  302.6 7.2 %multiply_reduce_fusion.3 = (f32[3,1024]{1,0:T(4,128)S(1)}, f32[3,1024,1024]{1,2,0:T(8,128)}) fusion(f32[3,1024,1024]{1,2,0:T(8,128)S(1)} %fusion.160, f32[3,1024]{1,0:T(4,128)S(1)} %dynamic-slice_bitcast_fusion.2, pred[1024,1024]{0,1:T(8,128)(4,1)S(1)} %fusion.161, bf16[2,1024,3,64]{1,3,2,0:T(8,128)(2,1)S(1)} %copy-done.11, s32[]{:T(128)S(6)} %copy.109, ...), kind=kOutput, calls=%fused_computation.27.clone.1 | convolution fusion | flops 418378752 | bytes 27030528 | tf_op jit(solution)/shard_map/while/body/eval_jaxpr/qhd,khd->hqk/dot_general | solution.py:74
  309.8 7.0 multiply_convert_fusion.3
  316.8 2.0 fusion.163
  321.1 1.8 fusion.161
  323.0 1.8 fusion.160
  324.8 3.7 fusion.164
  328.6 7.2 %multiply_reduce_fusion.3 = (f32[3,1024]{1,0:T(4,128)S(1)}, f32[3,1024,1024]{1,2,0:T(8,128)}) fusion(f32[3,1024,1024]{1,2,0:T(8,128)S(1)} %fusion.160, f32[3,1024]{1,0:T(4,128)S(1)} %dynamic-slice_bitcast_fusion.2, pred[1024,1024]{0,1:T(8,128)(4,1)S(1)} %fusion.161, bf16[2,1024,3,64]{1,3,2,0:T(8,128)(2,1)S(1)} %copy-done.11, s32[]{:T(128)S(6)} %copy.109, ...), kind=kOutput, calls=%fused_computation.27.clone.1 | convolution fusion | flops 418378752 | bytes 27030528 | tf_op jit(solution)/shard_map/while/body/eval_jaxpr/qhd,khd->hqk/dot_general | solution.py:74
  335.8 7.0 multiply_convert_fusion.3
  342.9 2.0 fusion.163
  347.3 2.0 copy.68
  350.9 1.9 copy.69
  356.8 6.2 bitcast_convert_fusion
  363.2 6.9 fusion.108
  370.5 8.6 %fusion.98 = f32[768,768]{1,0:T(8,128)} fusion(bf16[2048,768]{1,0:T(8,128)(2,1)} %copy-done.68, f32[768]{0:T(1024)S(1)} %copy-done.64, f32[768]{0:T(1024)S(1)} %copy-done.51, f32[2048]{0:T(1024)S(1)} %copy-done.45, bf16[2048,768]{1,0:T(8,128)(2,1)} %all-reduce.14.cloned.1.call-done, bf16[2048,768]{1,0:T(8,128)(2,1)} %param.21, f32[2048]{0:T(1024)S(1)} %copy-done.30, ...), kind=kOutput, calls=%fused_computation.161 | convolution fusion | flops 2430074880 | bytes 11822080 | tf_op jit(solution)/shard_map/td,tf->df/dot_general | solution.py:142
  379.2 7.6 %fusion.85 = f32[768,3,192]{2,0,1:T(8,128)} fusion(bf16[2048,3,192]{0,2,1:T(8,128)(2,1)} %constant_dynamic-update-slice_fusion, bf16[2048,768]{1,0:T(8,128)(2,1)} %param.21, f32[768]{0:T(1024)S(1)} %copy-done.66, f32[768]{0:T(1024)S(1)} %copy-done.53, f32[2048]{0:T(1024)S(1)} %copy-done.42, f32[2048]{0:T(1024)S(1)} %copy-done.28), kind=kOutput, calls=%fused_computation.129 | convolution fusion | flops 1821376512 | bytes 7297024 | tf_op jit(solution)/shard_map/td,tje->dje/dot_general | solution.py:173
  389.3 1.6 copy.81
  391.0 92.2 %all-reduce.18.cloned.1.call-done = (bf16[2048,768]{1,0:T(8,128)(2,1)}, bf16[2048,768]{1,0:T(8,128)(2,1)}) async-done(((bf16[2048,768]{1,0:T(8,128)(2,1)}, bf16[2048,768]{1,0:T(8,128)(2,1)}), (bf16[2048,768]{1,0:T(8,128)(2,1)}, bf16[2048,768]{1,0:T(8,128)(2,1)})) %all-reduce.18.cloned.1.call-update) | async-done | bytes 6291472 | tf_op jit(solution)/shard_map/psum | solution.py:134
  483.2 4.2 convert_reduce_fusion
  487.5 5.1 fusion.76
  492.6 37.7 %all-reduce.8 = (f32[768]{0:T(1024)S(1)}, f32[768]{0:T(1024)S(1)}, f32[2,192]{1,0:T(2,128)S(1)}, f32[768]{0:T(1024)S(1)}, f32[768]{0:T(1024)S(1)}, /*index=5*/f3...) all-reduce(f32[768]{0:T(1024)S(1)} %get-tuple-element.196, ...), channel_id=2, replica_groups=mesh['dp'=8,'mp'=4] {'dp'}, use_global_device_ids=true, to_apply=%region_20.21.clone | all-reduce | flops 5760 | bytes 46080
  535.0 12.4 %add_add_fusion.2 = (f32[2048,768]{1,0:T(8,128)}, bf16[2048,768]{1,0:T(8,128)(2,1)}) fusion(f32[2048,768]{1,0:T(8,128)} %copy-done.7, bf16[2048,768]{1,0:T(8,128)(2,1)} %param.21, bf16[2048,768]{1,0:T(8,128)(2,1)} %get-tuple-element.255, f32[2048]{0:T(1024)S(1)} %negate_multiply_fusion.1, f32[2048]{0:T(1024)S(1)} %multiply_multiply_fusion.5, ...), kind=kLoop, calls=%fused_computation.104 | loop fusion | flops 26738688 | bytes 28353536 | tf_op jit(solution)/shard_map/add | solution.py:181
  547.4 9.7 %reduce-scatter.12.cloned.1.call-done = f32[768,96]{0,1:T(8,128)} async-done(((f32[768,768]{0,1:T(8,128)}), f32[768,96]{0,1:T(8,128)}) %reduce-scatter.12.cloned.1.call-update) | async-done | bytes 294928 | tf_op jit(solution)/shard_map/reduce_scatter | solution.py:193
  557.1 72.4 %reduce-scatter.10.cloned.1.call-done = f32[96,768]{1,0:T(8,128)} async-done(((f32[768,768]{1,0:T(8,128)}), f32[96,768]{1,0:T(8,128)}) %reduce-scatter.10.cloned.1.call-update) | async-done | bytes 294928 | tf_op jit(solution)/shard_map/reduce_scatter | solution.py:191
  629.5 72.4 %reduce-scatter.8.cloned.1.call-done = f32[96,3,192]{2,0,1:T(8,128)} async-done(((f32[768,3,192]{2,0,1:T(8,128)}), f32[96,3,192]{2,0,1:T(8,128)}) %reduce-scatter.8.cloned.1.call-update) | async-done | bytes 221200 | tf_op jit(solution)/shard_map/reduce_scatter | solution.py:185
  (228 shorter events, 33.3 us)
Async XLA Ops:
  7.2 162.9 %copy-start = (bf16[768,768]{1,0:T(8,128)(2,1)S(1)}, bf16[768,768]{1,0:T(8,128)(2,1)}, u32[]{:S(2)}) copy-start(bf16[768,768]{1,0:T(8,128)(2,1)} %param.35) | copy-start | bytes 3538948
  7.2 6.2 copy-start.52
  7.2 6.2 copy-start.65
  7.2 6.2 copy-start.63
  7.2 150.4 %all-reduce.14.cloned.1.call-start = ((), (), s32[]{:S(2)}) async-start(), calls=%async_computation.4 | async-start | bytes 6291456 | tf_op jit(solution)/shard_map/psum | solution.py:127
  7.3 6.1 copy-start.2
  9.8 5.9 copy-start.27
  22.2 9.1 %copy-start.34 = (s32[2,1024]{1,0:T(2,128)S(1)}, s32[2,1024]{1,0:T(2,128)}, u32[]{:S(2)}) copy-start(s32[2,1024]{1,0:T(2,128)} %param.24) | copy-start | bytes 24580
  22.2 9.1 %copy-start.35 = (s32[2,1024]{1,0:T(2,128)S(1)}, s32[2,1024]{1,0:T(2,128)}, u32[]{:S(2)}) copy-start(s32[2,1024]{1,0:T(2,128)} %param.22) | copy-start | bytes 24580
  39.9 7.4 %copy-start.21 = (bf16[2,1024,3,64]{1,3,2,0:T(8,128)(2,1)S(1)}, bf16[2,1024,3,64]{1,3,2,0:T(8,128)(2,1)}, u32[]{:S(2)}) copy-start(bf16[2,1024,3,64]{1,3,2,0:T(8,128)(2,1)} %get-tuple-element.431) | copy-start | bytes 2359300 | tf_op jit(solution)/shard_map/while
  47.3 6.9 copy-start.31
  64.1 7.4 %copy-start.21 = (bf16[2,1024,3,64]{1,3,2,0:T(8,128)(2,1)S(1)}, bf16[2,1024,3,64]{1,3,2,0:T(8,128)(2,1)}, u32[]{:S(2)}) copy-start(bf16[2,1024,3,64]{1,3,2,0:T(8,128)(2,1)} %get-tuple-element.431) | copy-start | bytes 2359300 | tf_op jit(solution)/shard_map/while
  71.5 6.9 copy-start.31
  82.4 75.2 %copy-start.38 = (f32[768]{0:T(1024)S(1)}, f32[768]{0:T(1024)}, u32[]{:S(2)}) copy-start(f32[768]{0:T(1024)} %param.30) | copy-start | bytes 9220
  86.3 177.3 %all-reduce.16.cloned.1.call-start = ((), (), s32[]{:S(2)}) async-start(), calls=%async_computation.5 | async-start | bytes 6291456 | tf_op jit(solution)/shard_map/psum | solution.py:144
  157.6 4.7 copy-start.5
  157.6 7.7 %copy-start.62 = (bf16[768,768]{1,0:T(8,128)(2,1)S(1)}, bf16[768,768]{1,0:T(8,128)(2,1)}, u32[]{:S(2)}) copy-start(bf16[768,768]{1,0:T(8,128)(2,1)} %param.33) | copy-start | bytes 3538948
  162.3 113.1 %copy-start.29 = (f32[2048]{0:T(1024)}, f32[2048]{0:T(1024)S(1)}, u32[]{:S(2)}) copy-start(f32[2048]{0:T(1024)S(1)} %broadcast_multiply_fusion) | copy-start | bytes 24580
  165.3 4.7 copy-start.43
  165.3 4.7 copy-start.24
  165.3 4.7 copy-start.58
  170.1 19.1 %copy-start.18 = (f32[2048,768]{1,0:T(8,128)}, f32[2048,768]{1,0:T(8,128)S(1)}, u32[]{:S(2)}) copy-start(f32[2048,768]{1,0:T(8,128)S(1)} %fusion.99) | copy-start | bytes 18874372
  194.9 194.4 %reduce-scatter.14.cloned.1.call-start = ((), (), s32[]{:S(2)}) async-start(), calls=%async_computation.9 | async-start | bytes 884736
  206.7 62.8 %copy-start.49 = (f32[2048]{0:T(1024)S(1)}, f32[2048]{0:T(1024)}, u32[]{:S(2)}) copy-start(f32[2048]{0:T(1024)} %copy-done.48) | copy-start | bytes 24580
  206.7 62.8 %copy-start.39 = (f32[768]{0:T(1024)S(1)}, f32[768]{0:T(1024)}, u32[]{:S(2)}) copy-start(f32[768]{0:T(1024)} %param.30) | copy-start | bytes 9220
  206.7 62.8 %copy-start.44 = (f32[2048]{0:T(1024)S(1)}, f32[2048]{0:T(1024)}, u32[]{:S(2)}) copy-start(f32[2048]{0:T(1024)} %copy-done.43) | copy-start | bytes 24580
  206.7 62.8 %copy-start.50 = (f32[768]{0:T(1024)S(1)}, f32[768]{0:T(1024)}, u32[]{:S(2)}) copy-start(f32[768]{0:T(1024)} %param.31) | copy-start | bytes 9220
  263.6 5.9 copy-start.4
  263.6 5.9 copy-start.6
  263.6 6.5 copy-start.9
  269.5 5.9 copy-start.25
  280.0 5.0 copy-start.26
  285.0 9.9 %copy-start.33 = (f32[2,3,1024]{2,1,0:T(4,128)S(1)}, f32[2,3,1024]{2,1,0:T(4,128)}, u32[]{:S(2)}) copy-start(f32[2,3,1024]{2,1,0:T(4,128)} %get-tuple-element.459) | copy-start | bytes 73732
  285.0 9.9 %copy-start.36 = (s32[2,1024]{1,0:T(2,128)S(1)}, s32[2,1024]{1,0:T(2,128)}, u32[]{:S(2)}) copy-start(s32[2,1024]{1,0:T(2,128)} %param.22) | copy-start | bytes 24580
  285.0 9.9 %copy-start.37 = (s32[2,1024]{1,0:T(2,128)S(1)}, s32[2,1024]{1,0:T(2,128)}, u32[]{:S(2)}) copy-start(s32[2,1024]{1,0:T(2,128)} %get-tuple-element.524) | copy-start | bytes 24580
  289.0 194.2 %all-reduce.18.cloned.1.call-start = ((), (), s32[]{:S(2)}) async-start(), calls=%async_computation.10 | async-start | bytes 12582912 | tf_op jit(solution)/shard_map/psum | solution.py:134
  302.5 7.2 %copy-start.13 = (bf16[2,1024,3,64]{1,3,2,0:T(8,128)(2,1)}, bf16[2,1024,3,64]{1,3,2,0:T(8,128)(2,1)S(1)}, u32[]{:S(2)}) copy-start(bf16[2,1024,3,64]{1,3,2,0:T(8,128)(2,1)S(1)} %fusion.164) | copy-start | bytes 2359300 | tf_op jit(solution)/shard_map/while
  309.8 7.1 copy-start.19
  328.6 7.2 %copy-start.13 = (bf16[2,1024,3,64]{1,3,2,0:T(8,128)(2,1)}, bf16[2,1024,3,64]{1,3,2,0:T(8,128)(2,1)S(1)}, u32[]{:S(2)}) copy-start(bf16[2,1024,3,64]{1,3,2,0:T(8,128)(2,1)S(1)} %fusion.164) | copy-start | bytes 2359300 | tf_op jit(solution)/shard_map/while
  335.8 7.0 copy-start.19
  347.3 6.1 copy-start.14
  363.1 7.4 %copy-start.30 = (f32[2048]{0:T(1024)S(1)}, f32[2048]{0:T(1024)}, u32[]{:S(2)}) copy-start(f32[2048]{0:T(1024)} %copy-done.29) | copy-start | bytes 24580
  363.1 7.4 %copy-start.40 = (f32[768]{0:T(1024)S(1)}, f32[768]{0:T(1024)}, u32[]{:S(2)}) copy-start(f32[768]{0:T(1024)} %param.30) | copy-start | bytes 9220
  363.1 7.4 %copy-start.45 = (f32[2048]{0:T(1024)S(1)}, f32[2048]{0:T(1024)}, u32[]{:S(2)}) copy-start(f32[2048]{0:T(1024)} %copy-done.43) | copy-start | bytes 24580
  363.1 7.4 %copy-start.51 = (f32[768]{0:T(1024)S(1)}, f32[768]{0:T(1024)}, u32[]{:S(2)}) copy-start(f32[768]{0:T(1024)} %param.31) | copy-start | bytes 9220
  363.1 7.4 %copy-start.64 = (f32[768]{0:T(1024)S(1)}, f32[768]{0:T(1024)}, u32[]{:S(2)}) copy-start(f32[768]{0:T(1024)} %param.32) | copy-start | bytes 9220
  363.1 194.0 %reduce-scatter.12.cloned.1.call-start = ((), (), s32[]{:S(2)}) async-start(), calls=%async_computation.8 | async-start | bytes 2654208 | tf_op jit(solution)/shard_map/reduce_scatter | solution.py:193
  370.1 9.1 %copy-start.28 = (f32[2048]{0:T(1024)S(1)}, f32[2048]{0:T(1024)}, u32[]{:S(2)}) copy-start(f32[2048]{0:T(1024)} %copy-done.27) | copy-start | bytes 24580
  370.1 9.1 %copy-start.42 = (f32[2048]{0:T(1024)S(1)}, f32[2048]{0:T(1024)}, u32[]{:S(2)}) copy-start(f32[2048]{0:T(1024)} %copy-done.41) | copy-start | bytes 24580
  370.1 9.1 %copy-start.53 = (f32[768]{0:T(1024)S(1)}, f32[768]{0:T(1024)}, u32[]{:S(2)}) copy-start(f32[768]{0:T(1024)} %param.25) | copy-start | bytes 9220
  370.1 9.1 %copy-start.66 = (f32[768]{0:T(1024)S(1)}, f32[768]{0:T(1024)}, u32[]{:S(2)}) copy-start(f32[768]{0:T(1024)} %param.26) | copy-start | bytes 9220
  370.1 259.3 %reduce-scatter.10.cloned.1.call-start = ((), (), s32[]{:S(2)}) async-start(), calls=%async_computation.7 | async-start | bytes 2654208 | tf_op jit(solution)/shard_map/reduce_scatter | solution.py:191
  379.1 7.7 %copy-start.67 = (u32[32]{0:T(128)S(1)}, u32[32]{0:T(128)}, u32[]{:S(2)}) copy-start(u32[32]{0:T(128)} %constant.138) | copy-start | bytes 388
  379.1 9.9 %copy-start.17 = (bf16[2,1024,3,64]{1,3,2,0:T(8,128)(2,1)S(1)}, bf16[2,1024,3,64]{1,3,2,0:T(8,128)(2,1)}, u32[]{:S(2)}) copy-start(bf16[2,1024,3,64]{1,3,2,0:T(8,128)(2,1)} %get-tuple-element.128) | copy-start | bytes 2359300
  379.1 322.7 %reduce-scatter.8.cloned.1.call-start = ((), (), s32[]{:S(2)}) async-start(), calls=%async_computation.6 | async-start | bytes 2654208 | tf_op jit(solution)/shard_map/reduce_scatter | solution.py:185
  386.8 100.6 %copy-start.47 = (f32[2048]{0:T(1024)S(1)}, f32[2048]{0:T(1024)}, u32[]{:S(2)}) copy-start(f32[2048]{0:T(1024)} %copy-done.46) | copy-start | bytes 24580
  483.2 4.3 copy-start.8
  483.2 9.4 %copy-start.54 = (f32[768]{0:T(1024)S(1)}, f32[768]{0:T(1024)}, u32[]{:S(2)}) copy-start(f32[768]{0:T(1024)} %get-tuple-element.198) | copy-start | bytes 9220
  483.2 9.4 %copy-start.55 = (f32[768]{0:T(1024)S(1)}, f32[768]{0:T(1024)}, u32[]{:S(2)}) copy-start(f32[768]{0:T(1024)} %get-tuple-element.194) | copy-start | bytes 9220
  483.2 9.4 %copy-start.56 = (f32[768]{0:T(1024)S(1)}, f32[768]{0:T(1024)}, u32[]{:S(2)}) copy-start(f32[768]{0:T(1024)} %get-tuple-element.259) | copy-start | bytes 9220
  483.2 9.4 %copy-start.57 = (f32[768]{0:T(1024)S(1)}, f32[768]{0:T(1024)}, u32[]{:S(2)}) copy-start(f32[768]{0:T(1024)} %get-tuple-element.271) | copy-start | bytes 9220
  483.2 9.5 %copy-start.60 = (f32[768]{0:T(1024)S(1)}, f32[768]{0:T(1024)}, u32[]{:S(2)}) copy-start(f32[768]{0:T(1024)} %get-tuple-element.256) | copy-start | bytes 9220
  483.2 51.8 %copy-start.59 = (f32[768]{0:T(1024)S(1)}, f32[768]{0:T(1024)}, u32[]{:S(2)}) copy-start(f32[768]{0:T(1024)} %param.36) | copy-start | bytes 9220
  535.0 166.8 %copy-start.1 = (bf16[768,768]{1,0:T(8,128)(2,1)S(1)}, bf16[768,768]{1,0:T(8,128)(2,1)}, u32[]{:S(2)}) copy-start(bf16[768,768]{1,0:T(8,128)(2,1)} %param.35) | copy-start | bytes 3538948
  (23 other events, 40.3 us)
Sparse Core Ops, SparseCore 0:
  86.4 71.1 all-reduce.13
  195.0 68.5 all-reduce.15
  289.1 62.6 reduce-scatter.13
  363.2 119.9 all-reduce.17
  487.5 69.5 reduce-scatter.11
  561.4 68.0 reduce-scatter.9
  633.9 67.8 reduce-scatter.7
where the time goes:
time: 713 us; the launch traced here: 709 us
  waiting for transfers between devices  375 us (53%)
  matrix products  131 us (18%)
  other arithmetic  94.4 us (13%)
  local copies, waits for them, and re-layouts  52.5 us (7%)
  blocking collectives  37.7 us (5%)
  between operations  16.6 us (2%)
    psum x1, waiting for transfers between devices, body(): lax.psum(mlp_part.astype(jnp.bfloat16), 'mp').astype(jnp.float32) + b_down  92.2 us
    reduce_scatter x1, waiting for transfers between devices, body(): lax.psum_scatter(grad_w_up, 'dp', scatter_dimension=0, tiled=True)  72.4 us
    reduce_scatter x1, waiting for transfers between devices, body(): lax.psum_scatter(grad_w_qkv, 'dp', scatter_dimension=0, tiled=True)  72.4 us
    psum x1, waiting for transfers between devices, body(): lax.psum(attn_part.astype(jnp.bfloat16), 'mp').astype(jnp.float32) + b_out  71.2 us
    psum x1, waiting for transfers between devices, body(): lax.psum(normed_two_grad.astype(jnp.bfloat16), 'mp').astype(jnp.float32)  56.9 us
    unnamed x1, blocking collectives  37.7 us
    reduce_sum x4, other arithmetic, norm_apply(): return layer_norm(values) * norm_gain + norm_bias  20.4 us
    dot_general x1, matrix products, body(): jnp.einsum('td,fd->tf', cotangent, w_down, preferred_element_type=jnp.flo...  19.1 us
  transfers between devices with their start and end apart: 7, of which 6 were waited for; matrix products, arithmetic and copies ran while one was open for 19% of the time, Pallas kernels for 0%

commit v1 on v0

v1 whole, which is shorter than its diff:
```python
import functools

import jax
import jax.numpy as jnp
from jax import lax
from jax.experimental import pallas as pl
from jax.experimental.pallas import tpu as pltpu
from jax.sharding import PartitionSpec as P

HD = 64
QB = 128
MASKED = -1e30
EPS = 1e-05
LOG2E = 1.4426950408889634
F32 = jnp.float32
BF16 = jnp.bfloat16
NT = (((1,), (1,)), ((), ()))
NN = (((1,), (0,)), ((), ()))
TN = (((0,), (0,)), ((), ()))


def mm(a, b, dims):
    return lax.dot_general(a, b, dims, preferred_element_type=F32)


def params(mib):
    return pltpu.CompilerParams(vmem_limit_bytes=mib * 1024 * 1024)


def cost(flops, traffic, trans=0):
    return pl.CostEstimate(flops=int(flops), bytes_accessed=int(traffic), transcendentals=int(trans))


def whole(shape):
    return pl.BlockSpec(shape, lambda *ids: (0,) * len(shape))


def rows(tile, width):
    return pl.BlockSpec((tile, width), lambda i, *rest: (i, 0))


def sds(shape, dtype):
    return jax.ShapeDtypeStruct(shape, dtype)


def norm_stats(values):
    average = jnp.mean(values, -1, keepdims=True)
    centered = values - average
    variance = jnp.mean(centered * centered, -1, keepdims=True)
    scale = lax.rsqrt(variance + EPS)
    return centered * scale, scale


def norm_back(unit, scale, upstream):
    first = jnp.mean(upstream, -1, keepdims=True)
    second = jnp.mean(upstream * unit, -1, keepdims=True)
    return scale * (upstream - first - unit * second)


def add_rows(ref, values, first):
    total = jnp.sum(values, 0, keepdims=True)

    @pl.when(first)
    def _():
        ref[...] = total

    @pl.when(jnp.logical_not(first))
    def _():
        ref[...] += total


def add_to(ref, values, first):
    @pl.when(first)
    def _():
        ref[...] = values

    @pl.when(jnp.logical_not(first))
    def _():
        ref[...] += values


def project_kernel(x_ref, gain_ref, bias_ref, wt_ref, qkv_bias_ref, n1_ref, q_ref, k_ref, v_ref):
    unit, _ = norm_stats(x_ref[...].astype(F32))
    normed = (unit * gain_ref[...] + bias_ref[...]).astype(BF16)
    n1_ref[...] = normed
    width = q_ref.shape[1]
    for place, out in enumerate((q_ref, k_ref, v_ref)):
        cols = slice(place * width, (place + 1) * width)
        out[...] = (mm(normed, wt_ref[cols, :], NT) + qkv_bias_ref[:, cols]).astype(BF16)


def project(x, gain, bias, wt, qkv_bias):
    tokens, d = x.shape
    width = wt.shape[0] // 3
    tile = min(512, tokens)
    return pl.pallas_call(
        project_kernel,
        grid=(tokens // tile,),
        in_specs=[rows(tile, d), whole((1, d)), whole((1, d)), whole(wt.shape), whole((1, 3 * width))],
        out_specs=[rows(tile, d)] + [rows(tile, width)] * 3,
        out_shape=[sds((tokens, d), BF16)] + [sds((tokens, width), BF16)] * 3,
        compiler_params=params(40),
        cost_estimate=cost(6 * tokens * d * width, tokens * (4 * d + 6 * width) + 6 * d * width),
        name="norm_project",
    )(x, gain, bias, wt, qkv_bias)


def stack_pair(values):
    lane = lax.broadcasted_iota(jnp.int32, values.shape, 1)
    zero = jnp.zeros_like(values)
    return jnp.concatenate(
        [jnp.where(lane < HD, values, zero), jnp.where(lane >= HD, values, zero)], 0
    )


def mask_bias(code_ref, low, high, start, query_start):
    codes = code_ref[pl.ds(start, QB), :]
    key_at = lax.broadcasted_iota(jnp.int32, (QB, QB), 0) + start
    query_at = lax.broadcasted_iota(jnp.int32, (QB, QB), 1) + query_start
    allowed = ((codes >= low) & (codes <= high)) | (key_at == query_at)
    bias = jnp.where(allowed, jnp.float32(0), jnp.float32(MASKED))
    return jnp.concatenate([bias, bias], 1)


def attend_kernel(
    start_ref, count_ref, q_ref, k_ref, v_ref, code_ref, low_ref, high_ref, w_ref,
    ctx_ref, part_ref, lse_ref, acc_ref, stat_ref,
):
    sequence, block = pl.program_id(0), pl.program_id(1)
    place = sequence * pl.num_programs(1) + block
    pairs = q_ref.shape[1] // QB
    stacked = [stack_pair(q_ref[:, p * QB : (p + 1) * QB]) for p in range(pairs)]
    low, high = low_ref[0], high_ref[0]
    acc_ref[...] = jnp.zeros_like(acc_ref)
    stat_ref[0] = jnp.full(stat_ref.shape[1:], MASKED, F32)
    stat_ref[1] = jnp.zeros(stat_ref.shape[1:], F32)

    def step(turn, carry):
        start = pl.multiple_of(start_ref[place] + turn * QB, 16)
        bias = mask_bias(code_ref, low, high, start, block * QB)
        for p in range(pairs):
            cols = slice(p * QB, (p + 1) * QB)
            scores = mm(k_ref[pl.ds(start, QB), cols], stacked[p], NT) * (0.125 * LOG2E) + bias
            old = stat_ref[0, p : p + 1, :]
            top = jnp.maximum(old, jnp.max(scores, 0, keepdims=True))
            shrink = jnp.exp2(old - top)
            weights = jnp.exp2(scores - top)
            stat_ref[0, p : p + 1, :] = top
            stat_ref[1, p : p + 1, :] = stat_ref[1, p : p + 1, :] * shrink + jnp.sum(
                weights, 0, keepdims=True
            )
            acc_ref[p] = acc_ref[p] * shrink + mm(
                v_ref[pl.ds(start, QB), cols], weights.astype(BF16), TN
            )
        return carry

    lax.fori_loop(0, count_ref[place], step, 0)
    row = lax.broadcasted_iota(jnp.int32, (QB, QB), 0)
    for p in range(pairs):
        total = stat_ref[1, p : p + 1, :]
        lse_ref[0, p : p + 1, :] = stat_ref[0, p : p + 1, :] + jnp.log2(total)
        scaled = acc_ref[p] * (1.0 / total)
        both = jnp.where(row < HD, scaled[:, :QB], scaled[:, QB:])
        ctx_ref[:, p * QB : (p + 1) * QB] = both.T.astype(BF16)
    part_ref[...] = mm(ctx_ref[...], w_ref[...], NN).astype(BF16)


def attend(starts, counts, q, k, v, codes, low, high, w_out):
    tokens, width = q.shape
    sequences = codes.shape[0]
    length = tokens // sequences
    blocks = length // QB
    d = w_out.shape[1]
    pairs = width // QB
    block = lambda s, i, *rest: (s * blocks + i, 0)
    rank3 = lambda s, i, *rest: (s * blocks + i, 0, 0)
    whole_sequence = pl.BlockSpec((length, width), lambda s, i, *rest: (s, 0))
    return pl.pallas_call(
        attend_kernel,
        grid_spec=pltpu.PrefetchScalarGridSpec(
            num_scalar_prefetch=2,
            grid=(sequences, blocks),
            in_specs=[
                pl.BlockSpec((QB, width), block),
                whole_sequence,
                whole_sequence,
                pl.BlockSpec((None, length, QB), lambda s, i, *rest: (s, 0, 0)),
                pl.BlockSpec((1, 1, QB), rank3),
                pl.BlockSpec((1, 1, QB), rank3),
                whole(w_out.shape),
            ],
            out_specs=[
                pl.BlockSpec((QB, width), block),
                pl.BlockSpec((QB, d), block),
                pl.BlockSpec((1, 8, 2 * QB), rank3),
            ],
            scratch_shapes=[
                pltpu.VMEM((pairs, QB, 2 * QB), F32),
                pltpu.VMEM((2, 8, 2 * QB), F32),
            ],
        ),
        out_shape=[
            sds((tokens, width), BF16),
            sds((tokens, d), BF16),
            sds((sequences * blocks, 8, 2 * QB), F32),
        ],
        compiler_params=params(40),
        cost_estimate=cost(12e9, 10e6),
        name="attend_forward",
    )(starts, counts, q, k, v, codes, low, high, w_out)


def attend_back_kernel(
    start_ref, count_ref, q_ref, k_ref, v_ref, ctx_ref, grad_ref, lse_ref, code_ref, low_ref, high_ref,
    dq_ref, dk_ref, dv_ref, dq_acc, dk_acc, dv_acc,
):
    sequence, block = pl.program_id(0), pl.program_id(1)
    place = sequence * pl.num_programs(1) + block
    pairs = q_ref.shape[1] // QB

    @pl.when(block == 0)
    def _():
        dk_acc[...] = jnp.zeros_like(dk_acc)
        dv_acc[...] = jnp.zeros_like(dv_acc)

    low, high = low_ref[0], high_ref[0]
    stacked, upstream, delta = [], [], []
    for p in range(pairs):
        cols = slice(p * QB, (p + 1) * QB)
        stacked.append(stack_pair(q_ref[:, cols]))
        upstream.append(stack_pair(grad_ref[:, cols]))
        turned = (ctx_ref[:, cols].astype(F32) * grad_ref[:, cols].astype(F32)).T
        delta.append(
            jnp.concatenate(
                [jnp.sum(turned[:HD], 0, keepdims=True), jnp.sum(turned[HD:], 0, keepdims=True)], 1
            )
        )
    dq_acc[...] = jnp.zeros_like(dq_acc)

    def step(turn, carry):
        start = pl.multiple_of(start_ref[place] + turn * QB, 16)
        here = pl.ds(start, QB)
        bias = mask_bias(code_ref, low, high, start, block * QB)
        for p in range(pairs):
            cols = slice(p * QB, (p + 1) * QB)
            keys = k_ref[here, cols]
            scores = mm(keys, stacked[p], NT) * (0.125 * LOG2E) + bias
            weights = jnp.exp2(scores - lse_ref[0, p : p + 1, :])
            prob_grad = mm(v_ref[here, cols], upstream[p], NT)
            score_grad = (weights * (prob_grad - delta[p])).astype(BF16)
            dv_acc[here, cols] += mm(weights.astype(BF16), upstream[p], NN)
            dk_acc[here, cols] += mm(score_grad, stacked[p], NN)
            dq_acc[p] += mm(keys, score_grad, TN)
        return carry

    lax.fori_loop(0, count_ref[place], step, 0)
    row = lax.broadcasted_iota(jnp.int32, (QB, QB), 0)
    for p in range(pairs):
        both = jnp.where(row < HD, dq_acc[p, :, :QB], dq_acc[p, :, QB:])
        dq_ref[:, p * QB : (p + 1) * QB] = (both.T * 0.125).astype(BF16)

    @pl.when(block == pl.num_programs(1) - 1)
    def _():
        dk_ref[...] = (dk_acc[...] * 0.125).astype(BF16)
        dv_ref[...] = dv_acc[...].astype(BF16)


def attend_back(starts, counts, q, k, v, ctx, grad, lse, codes, low, high):
    tokens, width = q.shape
    sequences = codes.shape[0]
    length = tokens // sequences
    blocks = length // QB
    pairs = width // QB
    block = pl.BlockSpec((QB, width), lambda s, i, *rest: (s * blocks + i, 0))
    rank3 = lambda s, i, *rest: (s * blocks + i, 0, 0)
    whole_sequence = pl.BlockSpec((length, width), lambda s, i, *rest: (s, 0))
    return pl.pallas_call(
        attend_back_kernel,
        grid_spec=pltpu.PrefetchScalarGridSpec(
            num_scalar_prefetch=2,
            grid=(sequences, blocks),
            in_specs=[
                block,
                whole_sequence,
                whole_sequence,
                block,
                block,
                pl.BlockSpec((1, 8, 2 * QB), rank3),
                pl.BlockSpec((None, length, QB), lambda s, i, *rest: (s, 0, 0)),
                pl.BlockSpec((1, 1, QB), rank3),
                pl.BlockSpec((1, 1, QB), rank3),
            ],
            out_specs=[block, whole_sequence, whole_sequence],
            scratch_shapes=[
                pltpu.VMEM((pairs, QB, 2 * QB), F32),
                pltpu.VMEM((length, width), F32),
                pltpu.VMEM((length, width), F32),
            ],
        ),
        out_shape=[sds((tokens, width), BF16)] * 3,
        compiler_params=params(40),
        cost_estimate=cost(24e9, 14e6),
        name="attend_backward",
    )(starts, counts, q, k, v, ctx, grad, lse, codes, low, high)


def gelu_parts(z):
    spread = jnp.exp2(z * z * (-0.5 * LOG2E))
    t = 1.0 / (1.0 + (0.3275911 * 0.7071067811865476) * jnp.abs(z))
    poly = t * (0.254829592 + t * (-0.284496736 + t * (1.421413741 + t * (-1.453152027 + t * 1.061405429))))
    tail = 0.5 * poly * spread
    return jnp.where(z >= 0, 1.0 - tail, tail), spread


def mlp_kernel(
    x_ref, part_a_ref, part_b_ref, b_out_ref, gain_ref, bias_ref, cot_ref,
    up_a_ref, up_b_ref, down_a_ref, down_b_ref, bup_a_ref, bup_b_ref,
    residual_ref, mlp_ref, n2g_ref, dup_ref, ddown_ref, dbup_ref, dgain_ref, dbias_ref, dbdown_ref,
):
    first = pl.program_id(0) == 0
    residual = (
        x_ref[...].astype(F32)
        + (part_a_ref[...].astype(F32) + part_b_ref[...].astype(F32))
        + b_out_ref[...]
    )
    residual_ref[...] = residual
    unit, _ = norm_stats(residual)
    normed = (unit * gain_ref[...] + bias_ref[...]).astype(BF16)
    cot = cot_ref[...]
    mlp_out, n2_grad = None, None
    for own, up_ref, down_ref, bup_ref in (
        (True, up_a_ref, down_a_ref, bup_a_ref),
        (False, up_b_ref, down_b_ref, bup_b_ref),
    ):
        z = mm(normed, up_ref[...], NN) + bup_ref[...]
        hidden_grad = mm(cot, down_ref[...], NT)
        phi, spread = gelu_parts(z)
        hidden = (z * phi).astype(BF16)
        slope = phi + z * spread * 0.3989422804014327
        grad = hidden_grad * slope
        up_grad = grad.astype(BF16)
        here = mm(hidden, down_ref[...], NN)
        mlp_out = here if mlp_out is None else mlp_out + here
        here = mm(up_grad, up_ref[...], NT)
        n2_grad = here if n2_grad is None else n2_grad + here
        if own:
            add_rows(dbup_ref, grad, first)
            add_to(dup_ref, mm(normed, up_grad, TN), first)
            add_to(ddown_ref, mm(cot, hidden, TN), first)
    mlp_ref[...] = mlp_out.astype(BF16)
    n2g_ref[...] = n2_grad.astype(BF16)
    add_rows(dgain_ref, n2_grad * unit, first)
    add_rows(dbias_ref, n2_grad, first)
    add_rows(dbdown_ref, cot.astype(F32), first)


def mlp(x, part_a, part_b, b_out, gain, bias, cot, up_a, up_b, down_a, down_b, bup_a, bup_b):
    tokens, d = x.shape
    f = up_a.shape[1]
    tile = min(256, tokens)
    tall = rows(tile, d)
    flat = whole((1, d))
    flat_f = whole((1, f))
    return pl.pallas_call(
        mlp_kernel,
        grid=(tokens // tile,),
        in_specs=[tall, tall, tall, flat, flat, flat, tall]
        + [whole((d, f))] * 2
        + [whole((f, d))] * 2
        + [flat_f] * 2,
        out_specs=[tall, tall, tall, whole((d, f)), whole((d, f)), flat_f, flat, flat, flat],
        out_shape=[
            sds((tokens, d), F32),
            sds((tokens, d), BF16),
            sds((tokens, d), BF16),
            sds((d, f), F32),
            sds((d, f), F32),
            sds((1, f), F32),
            sds((1, d), F32),
            sds((1, d), F32),
            sds((1, d), F32),
        ],
        compiler_params=params(56),
        cost_estimate=cost(20 * tokens * d * f, tokens * d * 16 + 16 * d * f, 4 * tokens * f),
        name="feed_forward",
    )(x, part_a, part_b, b_out, gain, bias, cot, up_a, up_b, down_a, down_b, bup_a, bup_b)


def middle_kernel(
    residual_ref, grad_a_ref, grad_b_ref, mlp_a_ref, mlp_b_ref, cot_ref, gain_ref, b_down_ref, ctx_ref, w_ref,
    out_ref, rgrad_ref, cgrad_ref, dw_ref, dbout_ref,
):
    first = pl.program_id(0) == 0
    residual = residual_ref[...]
    unit, scale = norm_stats(residual)
    upstream = (grad_a_ref[...].astype(F32) + grad_b_ref[...].astype(F32)) * gain_ref[...]
    rgrad = cot_ref[...].astype(F32) + norm_back(unit, scale, upstream)
    rgrad_ref[...] = rgrad
    agrad = rgrad.astype(BF16)
    cgrad_ref[...] = mm(agrad, w_ref[...], NT).astype(BF16)
    own = dw_ref.shape[1]
    add_to(dw_ref, mm(agrad, ctx_ref[:, :own], TN), first)
    add_rows(dbout_ref, rgrad, first)
    out_ref[...] = (
        residual + ((mlp_a_ref[...].astype(F32) + mlp_b_ref[...].astype(F32)) + b_down_ref[...])
    ).astype(BF16)


def middle(residual, grad_a, grad_b, mlp_a, mlp_b, cot, gain, b_down, ctx, w_out):
    tokens, d = residual.shape
    width = w_out.shape[0]
    own = width // 2
    tile = min(512, tokens)
    tall, flat = rows(tile, d), whole((1, d))
    return pl.pallas_call(
        middle_kernel,
        grid=(tokens // tile,),
        in_specs=[tall] * 6 + [flat] * 2 + [rows(tile, width), whole(w_out.shape)],
        out_specs=[tall, tall, rows(tile, width), whole((d, own)), flat],
        out_shape=[
            sds((tokens, d), BF16),
            sds((tokens, d), F32),
            sds((tokens, width), BF16),
            sds((d, own), F32),
            sds((1, d), F32),
        ],
        compiler_params=params(48),
        cost_estimate=cost(3 * tokens * d * width, tokens * d * 20),
        name="second_norm_back",
    )(residual, grad_a, grad_b, mlp_a, mlp_b, cot, gain, b_down, ctx, w_out)


def project_back_kernel(
    x_ref, n1_ref, dq_ref, dk_ref, dv_ref, wt_ref,
    n1g_ref, dwq_ref, dwk_ref, dwv_ref, dbq_ref, dbv_ref, dgain_ref, dbias_ref,
):
    first = pl.program_id(0) == 0
    width = dq_ref.shape[1]
    own = dwq_ref.shape[1]
    total = None
    for place, grad_ref in enumerate((dq_ref, dk_ref, dv_ref)):
        here = mm(grad_ref[...], wt_ref[place * width : (place + 1) * width, :], NN)
        total = here if total is None else total + here
    n1g_ref[...] = total.astype(BF16)
    unit, _ = norm_stats(x_ref[...].astype(F32))
    add_rows(dgain_ref, total * unit, first)
    add_rows(dbias_ref, total, first)
    normed = n1_ref[...]
    for grad_ref, out in ((dq_ref, dwq_ref), (dk_ref, dwk_ref), (dv_ref, dwv_ref)):
        add_to(out, mm(normed, grad_ref[:, :own], TN), first)
    add_rows(dbq_ref, dq_ref[:, :own].astype(F32), first)
    add_rows(dbv_ref, dv_ref[:, :own].astype(F32), first)


def project_back(x, n1, dq, dk, dv, wt):
    tokens, d = x.shape
    width = dq.shape[1]
    own = width // 2
    tile = min(512, tokens)
    tall, flat = rows(tile, d), whole((1, d))
    return pl.pallas_call(
        project_back_kernel,
        grid=(tokens // tile,),
        in_specs=[tall] * 2 + [rows(tile, width)] * 3 + [whole(wt.shape)],
        out_specs=[tall] + [whole((d, own))] * 3 + [whole((1, own))] * 2 + [flat] * 2,
        out_shape=[sds((tokens, d), BF16)]
        + [sds((d, own), F32)] * 3
        + [sds((1, own), F32)] * 2
        + [sds((1, d), F32)] * 2,
        compiler_params=params(48),
        cost_estimate=cost(9 * tokens * d * width, tokens * d * 12),
        name="project_back",
    )(x, n1, dq, dk, dv, wt)


def first_back_kernel(x_ref, grad_a_ref, grad_b_ref, rgrad_ref, gain_ref, out_ref):
    unit, scale = norm_stats(x_ref[...].astype(F32))
    upstream = (grad_a_ref[...].astype(F32) + grad_b_ref[...].astype(F32)) * gain_ref[...]
    out_ref[...] = rgrad_ref[...] + norm_back(unit, scale, upstream)


def first_back(x, grad_a, grad_b, rgrad, gain):
    tokens, d = x.shape
    tile = min(512, tokens)
    tall = rows(tile, d)
    return pl.pallas_call(
        first_back_kernel,
        grid=(tokens // tile,),
        in_specs=[tall] * 4 + [whole((1, d))],
        out_specs=tall,
        out_shape=sds((tokens, d), F32),
        compiler_params=params(32),
        cost_estimate=cost(0, tokens * d * 14),
        name="first_norm_back",
    )(x, grad_a, grad_b, rgrad, gain)


def swap(value, axis, size, bit):
    return lax.ppermute(value, axis, [(i, i ^ bit) for i in range(size)])


def scatter_sum(chunks, size, bits, dtype):
    me = lax.axis_index("dp")
    levels = size.bit_length() - 1
    value = chunks.reshape((2,) * levels + chunks.shape[1:])
    left = list(range(levels))
    for bit in bits:
        axis = left.index(levels - 1 - bit)
        mine = (me >> bit) & 1
        keep = lax.dynamic_index_in_dim(value, mine, axis, keepdims=False)
        give = lax.dynamic_index_in_dim(value, 1 - mine, axis, keepdims=False)
        got = swap(give.astype(dtype), "dp", size, 1 << bit)
        value = keep.astype(F32) + got.astype(F32)
        left.pop(axis)
    return value


def body(
    n_dp,
    n_mp,
    block_input,
    segment_ids,
    group_ids,
    padding,
    ln1_gain,
    ln1_bias,
    w_qkv,
    b_qv,
    w_out,
    b_out,
    ln2_gain,
    ln2_bias,
    w_up,
    b_up,
    w_down,
    b_down,
    cotangent,
):
    sequences, length = segment_ids.shape
    tokens, d = block_input.shape
    own = w_qkv.shape[2]
    f = w_up.shape[1]
    blocks = length // QB
    far = lambda value: swap(value, "mp", n_mp, 2)
    near = lambda value: swap(value, "mp", n_mp, 1)
    row = lambda value: value.reshape(1, -1)

    wt_own = jnp.transpose(w_qkv, (1, 2, 0))
    wt_other = far(wt_own.reshape(3 * own, d)).reshape(3, own, d)
    wt = jnp.concatenate([wt_own, wt_other], 1).reshape(6 * own, d)
    w_out_all = jnp.concatenate([w_out, far(w_out)], 0)
    small = far(jnp.concatenate([b_qv.reshape(-1), b_up]))
    b_q = jnp.concatenate([b_qv[0], small[:own]])
    b_v = jnp.concatenate([b_qv[1], small[own : 2 * own]])
    b_up_other = small[2 * own :]
    qkv_bias = jnp.concatenate([b_q, jnp.zeros_like(b_q), b_v])
    w_up_other = far(w_up)
    w_down_other = far(w_down)

    codes = jnp.where(padding == 0, segment_ids * 4 + group_ids, -1)
    low = segment_ids * 4
    high = low + group_ids
    earliest = segment_ids[:, ::QB, None]
    latest = segment_ids[:, QB - 1 :: QB, None]
    key_from = jnp.sum(segment_ids[:, None, :] < earliest, -1, dtype=jnp.int32) // 16 * 16
    key_to = jnp.sum(segment_ids[:, None, :] <= latest, -1, dtype=jnp.int32)
    counts = (key_to - key_from + QB - 1) // QB
    starts = jnp.minimum(key_from, length - counts * QB)
    starts, counts = starts.reshape(-1), counts.reshape(-1)
    code_cols = jnp.broadcast_to(codes[:, :, None], (sequences, length, QB))
    low = low.reshape(sequences * blocks, 1, QB)
    high = high.reshape(sequences * blocks, 1, QB)

    n1, q, k, v = project(block_input, row(ln1_gain), row(ln1_bias), wt, row(qkv_bias))
    ctx, part, lse = attend(starts, counts, q, k, v, code_cols, low, high, w_out_all)
    part_near = near(part)
    residual, mlp_a, n2g, dw_up, dw_down, db_up, dgain2, dbias2, db_down = mlp(
        block_input, part, part_near, row(b_out), row(ln2_gain), row(ln2_bias), cotangent,
        w_up, w_up_other, w_down, w_down_other, row(b_up), row(b_up_other),
    )
    n2g_near = near(n2g)
    mlp_near = near(mlp_a)
    block_output, rgrad, cgrad, dw_out, db_out = middle(
        residual, n2g, n2g_near, mlp_a, mlp_near, cotangent, row(ln2_gain), row(b_down), ctx, w_out_all
    )
    bits = list(range(n_dp.bit_length() - 1))
    piece = d // n_dp
    up_sum = scatter_sum(dw_up.reshape(n_dp, piece, f), n_dp, bits, BF16)
    down_sum = scatter_sum(dw_down.reshape(n_dp, piece, f), n_dp, bits[1:] + bits[:1], BF16)
    dq, dk, dv = attend_back(starts, counts, q, k, v, ctx, cgrad, lse, code_cols, low, high)
    n1g, dwq, dwk, dwv, db_q, db_v, dgain1, dbias1 = project_back(block_input, n1, dq, dk, dv, wt)
    n1g_near = near(n1g)
    input_grad = first_back(block_input, n1g, n1g_near, rgrad, row(ln1_gain))

    dw_attn = jnp.concatenate([dwq, dwk, dwv, dw_out], 1).reshape(n_dp, piece, 4 * own)
    attn_sum = scatter_sum(dw_attn, n_dp, bits, BF16)
    by_device = lambda value: value.reshape(n_dp, -1)
    vectors = jnp.concatenate(
        [by_device(value) for value in (dgain1, dbias1, dgain2, dbias2, db_out, db_down, db_up, db_q, db_v)], 1
    )
    vector_sum = scatter_sum(vectors, n_dp, bits, F32)
    norm_sum = vector_sum[: 4 * piece]
    norm_sum = norm_sum + near(norm_sum)
    rest = vector_sum[4 * piece :]
    tiny = own // n_dp
    fp = f // n_dp
    cut = 2 * piece + fp
    return (
        block_output,
        input_grad,
        norm_sum[:piece],
        norm_sum[piece : 2 * piece],
        attn_sum[:, : 3 * own].reshape(piece, 3, own),
        jnp.stack([rest[cut : cut + tiny], rest[cut + tiny : cut + 2 * tiny]]),
        attn_sum[:, 3 * own :].T,
        rest[:piece],
        norm_sum[2 * piece : 3 * piece],
        norm_sum[3 * piece :],
        up_sum,
        rest[2 * piece : cut],
        down_sum.T,
        rest[piece : 2 * piece],
    )


def solution(mesh):
    return jax.shard_map(
        functools.partial(body, mesh.shape["dp"], mesh.shape["mp"]),
        mesh=mesh,
        in_specs=(
            P("dp", None),
            P("dp", None),
            P("dp", None),
            P("dp", None),
            P(),
            P(),
            P(None, None, "mp"),
            P(None, "mp"),
            P("mp", None),
            P(),
            P(),
            P(),
            P(None, "mp"),
            P("mp"),
            P("mp", None),
            P(),
            P("dp", None),
        ),
        out_specs=(
            P("dp", None),
            P("dp", None),
            P("dp"),
            P("dp"),
            P("dp", None, "mp"),
            P(None, ("mp", "dp")),
            P("mp", "dp"),
            P("dp"),
            P("dp"),
            P("dp"),
            P("dp", "mp"),
            P(("mp", "dp")),
            P("mp", "dp"),
            P("dp"),
        ),
        check_vma=False,
    )
```

time: 713 us -> 363 us (0.51)
  waiting for transfers between devices: 375 us -> 124 us
  Pallas kernels: 0 us -> 176 us
  matrix products: 131 us -> 0 us
  other arithmetic: 94.4 us -> 9.71 us
  blocking collectives: 37.7 us -> 0 us
  starting transfers between devices: 0.54 us -> 23.1 us
  local copies, waits for them, and re-layouts: 52.5 us -> 31.1 us
  between operations: 16.6 us -> 1.34 us
    psum x3 -> x0, waiting for transfers between devices: 220 us -> none  [the longest x1 92.2 us: body(): lax.psum(mlp_part.astype(jnp.bfloat16), 'mp').astype(jnp.float32) + b_down]
    pallas_call x0 -> x7, Pallas kernels: none -> 176 us  [the longest x1 50 us: mlp(): pl.pallas_call(mlp_kernel, grid=(tokens // tile,), in_specs=[tall, tall,...]
    reduce_scatter x3 -> x0, waiting for transfers between devices: 154 us -> none  [the longest x1 72.4 us: body(): lax.psum_scatter(grad_w_up, 'dp', scatter_dimension=0, tiled=True)]
    dot_general x24 -> x0, matrix products: 127 us -> none  [the longest x1 19.1 us: body(): jnp.einsum('td,fd->tf', cotangent, w_down, preferred_element_type=jnp.flo...]
    ppermute x0 -> x22, waiting for transfers between devices: none -> 124 us  [swap(): return lax.ppermute(value, axis, [(i, i ^ bit) for i in range(size)])]
    reduce_sum x13 -> x1, other arithmetic: 52.1 us -> 0.92 us  [body(): key_to = jnp.sum(segment_ids[:, None, :] <= latest, -1, dtype=jnp.int32)]
    unnamed x1 -> x0, blocking collectives: 37.7 us -> none
    ppermute x0 -> x22, starting transfers between devices: none -> 23.1 us  [swap(): return lax.ppermute(value, axis, [(i, i ^ bit) for i in range(size)])]
  transfers between devices with their start and end apart: 7 -> 22, of which waited for: 6 -> 13; matrix products, arithmetic and copies ran while one was open for 19% -> 7% of each run, Pallas kernels for 0% -> 0%
where the time goes in v1:
time: 363 us; the launch traced here: 364 us
  Pallas kernels  176 us (48%)
  waiting for transfers between devices  124 us (34%)
  local copies, waits for them, and re-layouts  31.1 us (9%)
  starting transfers between devices  23.1 us (6%)
  other arithmetic  9.71 us (3%)
    ppermute x22, waiting for transfers between devices, swap(): return lax.ppermute(value, axis, [(i, i ^ bit) for i in range(size)])  124 us
    pallas_call x1, Pallas kernels, mlp(): pl.pallas_call(mlp_kernel, grid=(tokens // tile,), in_specs=[tall, tall,...  50 us
    pallas_call x1, Pallas kernels, attend_back(): pl.pallas_call(attend_back_kernel, grid_spec=pltpu.PrefetchScalarGridSpec...  41.7 us
    pallas_call x1, Pallas kernels, attend(): pl.pallas_call(attend_kernel, grid_spec=pltpu.PrefetchScalarGridSpec(num_...  35.7 us
    ppermute x22, starting transfers between devices, swap(): return lax.ppermute(value, axis, [(i, i ^ bit) for i in range(size)])  23.1 us
    pallas_call x1, Pallas kernels, project_back(): pl.pallas_call(project_back_kernel, grid=(tokens // tile,), in_specs=[tal...  19.3 us
    pallas_call x1, Pallas kernels, middle(): pl.pallas_call(middle_kernel, grid=(tokens // tile,), in_specs=[tall] * 6...  14.2 us
    unnamed x74, local copies, waits for them, and re-layouts  13 us
  transfers between devices with their start and end apart: 22, of which 13 were waited for; matrix products, arithmetic and copies ran while one was open for 7% of the time, Pallas kernels for 0%

profile of v1, /device:TPU:0, one launch (start us, length us, event | category | flops | bytes accessed | tf_op | source)
XLA Modules:
  0.0 364.3 jit_solution(2553419807229416237)
XLA Ops:
  0.7 0.8 reshape.130
  1.5 0.7 pad_maximum_fusion.2
  2.2 3.0 collective-permute-start.1
  5.2 2.0 collective-permute-start.2
  7.2 0.8 fusion.18
  7.9 0.8 slice.63
  8.7 0.8 slice.64
  9.5 0.9 convert_reduce_fusion
  10.6 0.7 compare_select_fusion
  11.4 1.0 constant_dynamic-update-slice_fusion.1
  12.4 0.7 reshape.125.gain_ref
  13.1 0.7 reshape.126.bias_ref
  14.0 18.8 %collective-permute-done.2 = bf16[192,768]{1,0:T(8,128)(2,1)S(1)} collective-permute-done((bf16[192,768]{1,0:T(8,128)(2,1)}, bf16[192,768]{1,0:T(8,128)(2,1)S(1)}, u32[]{:S(2)}, u32[]{:S(2)}) %collective-permute-start.2) | collective-permute-done | bytes 294944 | tf_op jit(solution)/shard_map/ppermute | solution.py:499
  32.8 0.8 copy-done.5
  33.8 2.4 copy-done.1
  36.2 7.0 %norm_project.1 = (bf16[2048,768]{1,0:T(8,128)(2,1)S(1)}, bf16[2048,384]{1,0:T(8,128)(2,1)S(1)}, bf16[2048,384]{1,0:T(8,128)(2,1)S(1)}, bf16[2048,384]{1,0:T(8,128)(2,1)S(1)}) custom-call(bf16[2048,768]{1,0:T(8,128)(2,1)S(1)} %copy-done.1, f32[1,768]{1,0:T(1,128)S(1)} %reshape.125.gain_ref, f32[1,768]{1,0:T(1,128)S(1)} %reshape.126.bias_ref, ...), custom_call_target="tpu_custom_call" | custom-call | flops 3623878656 | bytes 12779520 | tf_op jit(solution)/shard_map/norm_project/pallas_call | solution.py:96
  43.7 35.7 %attend_forward.1 = (bf16[2048,384]{1,0:T(8,128)(2,1)S(1)}, bf16[2048,768]{1,0:T(8,128)(2,1)S(1)}, f32[16,8,256]{2,1,0:T(8,128)S(1)}) custom-call(s32[16]{0:T(128)S(1)} %get-tuple-element.126.start_ref, s32[16]{0:T(128)S(1)} %get-tuple-element.127.count_ref, bf16[2048,384]{1,0:T(8,128)(2,1)S(1)} %get-tuple-element.46.q_ref, ...), custom_call_target="tpu_custom_call" | custom-call | flops 12000000000 | bytes 10000000 | tf_op jit(solution)/shard_map/attend_forward/pallas_call | solution.py:178
  80.1 1.6 collective-permute-start.5
  81.7 0.6 reshape.137.bup_a_ref
  82.3 0.6 reshape.135.gain_ref
  82.8 0.6 reshape.134.b_out_ref
  84.0 0.6 reshape.138.bup_b_ref
  84.6 23.8 %collective-permute-done.4.up_b_ref = bf16[768,768]{1,0:T(8,128)(2,1)S(1)} collective-permute-done((bf16[768,768]{1,0:T(8,128)(2,1)S(1)}, bf16[768,768]{1,0:T(8,128)(2,1)S(1)}, u32[]{:S(2)}, u32[]{:S(2)}) %collective-permute-start.4) | collective-permute-done | bytes 1179680 | tf_op jit(solution)/shard_map/ppermute | solution.py:499
  108.4 24.8 %collective-permute-done.5.down_b_ref = bf16[768,768]{1,0:T(8,128)(2,1)S(1)} collective-permute-done((bf16[768,768]{1,0:T(8,128)(2,1)S(1)}, bf16[768,768]{1,0:T(8,128)(2,1)S(1)}, u32[]{:S(2)}, u32[]{:S(2)}) %collective-permute-start.5) | collective-permute-done | bytes 1179680 | tf_op jit(solution)/shard_map/ppermute | solution.py:499
  133.2 1.0 copy-done.34
  134.2 50.0 %feed_forward.1 = (f32[2048,768]{1,0:T(8,128)}, bf16[2048,768]{1,0:T(8,128)(2,1)}, bf16[2048,768]{1,0:T(8,128)(2,1)}, f32[768,768]{1,0:T(8,128)}, f32[768,768]{1...) custom-call(bf16[2048,768]{1,0:T(8,128)(2,1)} %x_ref.7, ...), custom_call_target="tpu_custom_call" | custom-call | flops 24159191040 | bytes 34603008 | tf_op jit(solution)/shard_map/feed_forward/pallas_call | solution.py:364
  184.9 1.3 fusion.2
  186.3 2.2 fusion
  188.4 3.0 collective-permute-start.16
  191.8 9.8 %collective-permute-done.19 = bf16[2,2,96,768]{3,2,1,0:T(8,128)(2,1)} collective-permute-done((bf16[2,2,96,768]{3,2,1,0:T(8,128)(2,1)S(1)}, bf16[2,2,96,768]{3,2,1,0:T(8,128)(2,1)}, u32[]{:S(2)}, u32[]{:S(2)}) %collective-permute-start.19) | collective-permute-done | bytes 589856 | tf_op jit(solution)/shard_map/ppermute | solution.py:499
  201.7 1.6 bitcast_add_fusion.1
  203.3 1.8 collective-permute-start.20
  205.1 1.2 bitcast_add_fusion.2
  206.4 1.8 collective-permute-start.17
  208.2 10.6 %collective-permute-done.20 = bf16[2,96,768]{2,1,0:T(8,128)(2,1)S(1)} collective-permute-done((bf16[2,96,768]{2,1,0:T(8,128)(2,1)S(1)}, bf16[2,96,768]{2,1,0:T(8,128)(2,1)S(1)}, u32[]{:S(2)}, u32[]{:S(2)}) %collective-permute-start.20) | collective-permute-done | bytes 294944 | tf_op jit(solution)/shard_map/ppermute | solution.py:499
  219.0 2.1 collective-permute-start.21
  221.3 3.3 collective-permute-done.21
  224.6 0.7 fusion.6
  225.4 3.9 %collective-permute-done.18 = bf16[96,768]{1,0:T(8,128)(2,1)S(1)} collective-permute-done((bf16[96,768]{1,0:T(8,128)(2,1)S(1)}, bf16[96,768]{1,0:T(8,128)(2,1)S(1)}, u32[]{:S(2)}, u32[]{:S(2)}) %collective-permute-start.18) | collective-permute-done | bytes 147488 | tf_op jit(solution)/shard_map/ppermute | solution.py:499
  229.2 0.7 bitcast_add_fusion.8
  230.0 14.2 %second_norm_back.1 = (bf16[2048,768]{1,0:T(8,128)(2,1)}, f32[2048,768]{1,0:T(8,128)}, bf16[2048,384]{1,0:T(8,128)(2,1)S(1)}, f32[768,192]{1,0:T(8,128)S(1)}, f32[1,768]{1,0:T(1,128)S(1)}) custom-call(f32[2048,768]{1,0:T(8,128)} %get-tuple-element.50.residual_ref, bf16[2048,768]{1,0:T(8,128)(2,1)} %get-tuple-element.51.grad_a_ref, ...), custom_call_target="tpu_custom_call" | custom-call | flops 1811939328 | bytes 31457280 | tf_op jit(solution)/shard_map/second_norm_back/pallas_call | solution.py:415
  244.3 41.7 %attend_backward.1 = (bf16[2048,384]{1,0:T(8,128)(2,1)S(1)}, bf16[2048,384]{1,0:T(8,128)(2,1)S(1)}, bf16[2048,384]{1,0:T(8,128)(2,1)S(1)}) custom-call(s32[16]{0:T(128)S(1)} %get-tuple-element.126.start_ref, s32[16]{0:T(128)S(1)} %get-tuple-element.127.count_ref, bf16[2048,384]{1,0:T(8,128)(2,1)S(1)} %copy-done.13, bf16[2048,384]{1,0:T(8,128)(2,1)S(1)} %copy-done.15, ...), custom_call_target="tpu_custom_call" | custom-call | flops 24000000000 | bytes 14000000 | tf_op jit(solution)/shard_map/attend_backward/pallas_call | solution.py:277
  285.9 1.2 copy-done.11
  287.1 19.3 %project_back.1 = (bf16[2048,768]{1,0:T(8,128)(2,1)}, f32[768,192]{1,0:T(8,128)S(1)}, f32[768,192]{1,0:T(8,128)S(1)}, f32[768,192]{1,0:T(8,128)S(1)}, f32[1,192]...) custom-call(bf16[2048,768]{1,0:T(8,128)(2,1)} %x_ref.7, ...), custom_call_target="tpu_custom_call" | custom-call | flops 5435817984 | bytes 18874368 | tf_op jit(solution)/shard_map/project_back/pallas_call | solution.py:461
  307.1 0.7 reduce.17
  307.9 0.7 reduce.18
  308.9 2.2 collective-permute-start.9
  311.7 1.1 collective-permute-done.9
  313.0 2.1 collective-permute-start.13
  315.1 1.5 collective-permute-done.10
  317.2 4.0 %collective-permute-done.11 = f32[720]{0:T(1024)S(1)} collective-permute-done((f32[720]{0:T(1024)S(1)}, f32[720]{0:T(1024)S(1)}, u32[]{:S(2)}, u32[]{:S(2)}) %collective-permute-start.11) | collective-permute-done | bytes 2912 | tf_op jit(solution)/shard_map/ppermute | solution.py:499
  321.2 0.6 fusion.16
  321.8 6.0 %collective-permute-done.13 = bf16[2,2,96,768]{3,2,1,0:T(8,128)(2,1)} collective-permute-done((bf16[2,2,96,768]{3,2,1,0:T(8,128)(2,1)S(1)}, bf16[2,2,96,768]{3,2,1,0:T(8,128)(2,1)}, u32[]{:S(2)}, u32[]{:S(2)}) %collective-permute-start.13) | collective-permute-done | bytes 589856 | tf_op jit(solution)/shard_map/ppermute | solution.py:499
  327.8 1.4 copy.51
  329.5 1.8 collective-permute-start.14
  331.8 7.2 %collective-permute-done.14 = bf16[2,96,768]{1,2,0:T(8,128)(2,1)S(1)} collective-permute-done((bf16[2,96,768]{1,2,0:T(8,128)(2,1)S(1)}, bf16[2,96,768]{1,2,0:T(8,128)(2,1)S(1)}, u32[]{:S(2)}, u32[]{:S(2)}) %collective-permute-start.14) | collective-permute-done | bytes 294944 | tf_op jit(solution)/shard_map/ppermute | solution.py:499
  339.4 0.6 fusion.17
  340.0 8.7 %collective-permute-done.15 = bf16[96,768]{0,1:T(8,128)(2,1)S(1)} collective-permute-done((bf16[96,768]{0,1:T(8,128)(2,1)S(1)}, bf16[96,768]{0,1:T(8,128)(2,1)S(1)}, u32[]{:S(2)}, u32[]{:S(2)}) %collective-permute-start.15) | collective-permute-done | bytes 147488 | tf_op jit(solution)/shard_map/ppermute | solution.py:499
  348.8 0.7 slice.85
  349.5 1.8 copy.55
  351.3 0.6 slice_bitcast_fusion
  352.0 2.8 copy-done
  354.8 1.9 copy-done.3
  356.7 7.6 %first_norm_back.1 = f32[2048,768]{1,0:T(8,128)} custom-call(bf16[2048,768]{1,0:T(8,128)(2,1)S(1)} %copy-done.2, bf16[2048,768]{1,0:T(8,128)(2,1)S(1)} %copy-done.3, bf16[2048,768]{1,0:T(8,128)(2,1)} %collective-permute-done.8.grad_b_ref, f32[2048,768]{1,0:T(8,128)S(1)} %copy-done, f32[1,768]{1,0:T(1,128)S(1)} %reshape.125.gain_ref), custom_call_target="tpu_custom_call" | custom-call | bytes 22020096 | tf_op jit(solution)/shard_map/first_norm_back/pallas_call | solution.py:486
  (145 shorter events, 7.4 us)
Async XLA Ops:
  0.6 33.0 %copy-start.21 = (bf16[768,3,192]{0,2,1:T(8,128)(2,1)S(1)}, bf16[768,3,192]{0,2,1:T(8,128)(2,1)}, u32[]{:S(2)}) copy-start(bf16[768,3,192]{0,2,1:T(8,128)(2,1)} %param.23) | copy-start | bytes 2654212
  2.2 11.6 %collective-permute-start.1 = (f32[1152]{0:T(1024)S(1)}, f32[1152]{0:T(1024)S(1)}, u32[]{:S(2)}, u32[]{:S(2)}) collective-permute-start(f32[1152]{0:T(1024)S(1)} %pad_maximum_fusion.2), channel_id=1, source_target_pairs={{0,2},{1,3},{2,0},{3,1},{4,6},{5,7},{6,4},{7,5},{8,10},{9,11},{10,... | collective-permute-start | bytes 13832 | tf_op jit(solution)/shard_map/ppermute | solution.py:499
  5.2 28.5 %collective-permute-start = (bf16[576,768]{1,0:T(8,128)(2,1)}, bf16[576,768]{1,0:T(8,128)(2,1)S(1)}, u32[]{:S(2)}, u32[]{:S(2)}) collective-permute-start(bf16[576,768]{1,0:T(8,128)(2,1)} %bitcast.84), channel_id=1, source_target_pairs={{0,2},{1,3},{2,0},{3,1},{4,6},{5,7},{6,4},{7,5},{8,10},{9,11},{10,... | collective-permute-start | bytes 2654216 | tf_op jit(solution)/shard_map/ppermute | solution.py:499
  5.2 27.6 %collective-permute-start.2 = (bf16[192,768]{1,0:T(8,128)(2,1)}, bf16[192,768]{1,0:T(8,128)(2,1)S(1)}, u32[]{:S(2)}, u32[]{:S(2)}) collective-permute-start(bf16[192,768]{1,0:T(8,128)(2,1)} %param.25), channel_id=1, source_target_pairs={{0,2},{1,3},{2,0},{3,1},{4,6},{5,7},{6,4},{7,5},{8,10},{9,11},{10,... | collective-permute-start | bytes 884744 | tf_op jit(solution)/shard_map/ppermute | solution.py:499
  32.8 0.8 copy-start.5
  33.7 2.5 copy-start.1
  33.8 9.5 %copy-start.4 = (bf16[3,384,768]{2,1,0:T(8,128)(2,1)}, bf16[3,384,768]{2,1,0:T(8,128)(2,1)S(1)}, u32[]{:S(2)}) copy-start(bf16[3,384,768]{2,1,0:T(8,128)(2,1)S(1)} %pad_maximum_fusion.1) | copy-start | bytes 5308420
  36.2 7.4 %copy-start.6 = (bf16[384,768]{1,0:T(8,128)(2,1)S(1)}, bf16[384,768]{1,0:T(8,128)(2,1)}, u32[]{:S(2)}) copy-start(bf16[384,768]{1,0:T(8,128)(2,1)} %copy-done.5) | copy-start | bytes 1769476
  43.2 36.2 %copy-start.10 = (bf16[2048,768]{1,0:T(8,128)(2,1)}, bf16[2048,768]{1,0:T(8,128)(2,1)S(1)}, u32[]{:S(2)}) copy-start(bf16[2048,768]{1,0:T(8,128)(2,1)S(1)} %get-tuple-element.55.n1_ref) | copy-start | bytes 9437188
  43.3 36.2 %copy-start.12 = (bf16[2048,384]{1,0:T(8,128)(2,1)}, bf16[2048,384]{1,0:T(8,128)(2,1)S(1)}, u32[]{:S(2)}) copy-start(bf16[2048,384]{1,0:T(8,128)(2,1)S(1)} %get-tuple-element.46.q_ref) | copy-start | bytes 4718596
  43.3 36.2 %copy-start.14 = (bf16[2048,384]{1,0:T(8,128)(2,1)}, bf16[2048,384]{1,0:T(8,128)(2,1)S(1)}, u32[]{:S(2)}) copy-start(bf16[2048,384]{1,0:T(8,128)(2,1)S(1)} %get-tuple-element.47.k_ref) | copy-start | bytes 4718596
  43.3 36.2 %copy-start.16 = (bf16[2048,384]{1,0:T(8,128)(2,1)}, bf16[2048,384]{1,0:T(8,128)(2,1)S(1)}, u32[]{:S(2)}) copy-start(bf16[2048,384]{1,0:T(8,128)(2,1)S(1)} %get-tuple-element.48.v_ref) | copy-start | bytes 4718596
  43.6 35.9 %copy-start.31 = (bf16[768,768]{1,0:T(8,128)(2,1)S(1)}, bf16[768,768]{1,0:T(8,128)(2,1)}, u32[]{:S(2)}) copy-start(bf16[768,768]{1,0:T(8,128)(2,1)} %up_a_ref.1) | copy-start | bytes 3538948
  43.6 36.4 %copy-start.32 = (bf16[768,768]{1,0:T(8,128)(2,1)S(1)}, bf16[768,768]{1,0:T(8,128)(2,1)}, u32[]{:S(2)}) copy-start(bf16[768,768]{1,0:T(8,128)(2,1)} %down_a_ref.1) | copy-start | bytes 3538948
  43.6 38.0 %copy-start.22 = (f32[768]{0:T(1024)S(1)}, f32[768]{0:T(1024)}, u32[]{:S(2)}) copy-start(f32[768]{0:T(1024)} %param.30) | copy-start | bytes 9220
  43.7 38.6 %copy-start.23 = (f32[768]{0:T(1024)S(1)}, f32[768]{0:T(1024)}, u32[]{:S(2)}) copy-start(f32[768]{0:T(1024)} %param.27) | copy-start | bytes 9220
  43.7 39.2 %copy-start.24 = (f32[768]{0:T(1024)S(1)}, f32[768]{0:T(1024)}, u32[]{:S(2)}) copy-start(f32[768]{0:T(1024)} %param.26) | copy-start | bytes 9220
  43.7 39.7 %copy-start.25 = (f32[768]{0:T(1024)S(1)}, f32[768]{0:T(1024)}, u32[]{:S(2)}) copy-start(f32[768]{0:T(1024)} %param.28) | copy-start | bytes 9220
  79.5 54.8 %copy-start.9 = (bf16[2048,768]{1,0:T(8,128)(2,1)}, bf16[2048,768]{1,0:T(8,128)(2,1)S(1)}, u32[]{:S(2)}) copy-start(bf16[2048,768]{1,0:T(8,128)(2,1)S(1)} %get-tuple-element.49.part_a_ref) | copy-start | bytes 9437188
  79.5 104.7 %copy-start.18 = (f32[16,8,256]{2,1,0:T(8,128)}, f32[16,8,256]{2,1,0:T(8,128)S(1)}, u32[]{:S(2)}) copy-start(f32[16,8,256]{2,1,0:T(8,128)S(1)} %get-tuple-element.57.lse_ref) | copy-start | bytes 393220
  79.5 54.7 %collective-permute-start.3 = (bf16[2048,768]{1,0:T(8,128)(2,1)S(1)}, bf16[2048,768]{1,0:T(8,128)(2,1)}, u32[]{:S(2)}, u32[]{:S(2)}) collective-permute-start(bf16[2048,768]{1,0:T(8,128)(2,1)S(1)} %get-tuple-element.49.part_a_ref), channel_id=1, source_target_pairs={{0,1},{1,0},{2,3},{3,2},{4,5},{5,4},{6,7},{7,6},{8,9},{9,8},{10,11... | collective-permute-start | bytes 9437192 | tf_op jit(solution)/shard_map/ppermute | solution.py:499
  79.6 28.8 %collective-permute-start.4 = (bf16[768,768]{1,0:T(8,128)(2,1)S(1)}, bf16[768,768]{1,0:T(8,128)(2,1)S(1)}, u32[]{:S(2)}, u32[]{:S(2)}) collective-permute-start(bf16[768,768]{1,0:T(8,128)(2,1)S(1)} %copy-done.31), channel_id=1, source_target_pairs={{0,2},{1,3},{2,0},{3,1},{4,6},{5,7},{6,4},{7,5},{8,10},{9,11},{10,... | collective-permute-start | bytes 3538952 | tf_op jit(solution)/shard_map/ppermute | solution.py:499
  80.1 53.2 %collective-permute-start.5 = (bf16[768,768]{1,0:T(8,128)(2,1)S(1)}, bf16[768,768]{1,0:T(8,128)(2,1)S(1)}, u32[]{:S(2)}, u32[]{:S(2)}) collective-permute-start(bf16[768,768]{1,0:T(8,128)(2,1)S(1)} %copy-done.32), channel_id=1, source_target_pairs={{0,2},{1,3},{2,0},{3,1},{4,6},{5,7},{6,4},{7,5},{8,10},{9,11},{10,... | collective-permute-start | bytes 3538952 | tf_op jit(solution)/shard_map/ppermute | solution.py:499
  108.4 24.8 %copy-start.33 = (bf16[768,768]{1,0:T(8,128)(2,1)}, bf16[768,768]{1,0:T(8,128)(2,1)S(1)}, u32[]{:S(2)}) copy-start(bf16[768,768]{1,0:T(8,128)(2,1)S(1)} %collective-permute-done.4.up_b_ref) | copy-start | bytes 3538948
  133.2 1.0 copy-start.34
  184.2 7.2 %copy-start.26 = (f32[768]{0:T(1024)S(1)}, f32[768]{0:T(1024)}, u32[]{:S(2)}) copy-start(f32[768]{0:T(1024)} %param.32) | copy-start | bytes 9220
  184.2 7.2 %copy-start.30 = (f32[1,768]{1,0:T(1,128)S(1)}, f32[1,768]{1,0:T(1,128)}, u32[]{:S(2)}) copy-start(f32[1,768]{1,0:T(1,128)} %get-tuple-element.65) | copy-start | bytes 9220
  184.2 7.3 %copy-start.29 = (f32[1,768]{1,0:T(1,128)S(1)}, f32[1,768]{1,0:T(1,128)}, u32[]{:S(2)}) copy-start(f32[1,768]{1,0:T(1,128)} %get-tuple-element.66) | copy-start | bytes 9220
  184.3 7.4 %copy-start.28 = (f32[1,768]{1,0:T(1,128)S(1)}, f32[1,768]{1,0:T(1,128)}, u32[]{:S(2)}) copy-start(f32[1,768]{1,0:T(1,128)} %get-tuple-element.68) | copy-start | bytes 9220
  184.3 7.5 %copy-start.27 = (f32[1,768]{1,0:T(1,128)S(1)}, f32[1,768]{1,0:T(1,128)}, u32[]{:S(2)}) copy-start(f32[1,768]{1,0:T(1,128)} %get-tuple-element.69) | copy-start | bytes 9220
  184.3 45.7 %collective-permute-start.6 = (bf16[2048,768]{1,0:T(8,128)(2,1)}, bf16[2048,768]{1,0:T(8,128)(2,1)}, u32[]{:S(2)}, u32[]{:S(2)}) collective-permute-start(bf16[2048,768]{1,0:T(8,128)(2,1)} %get-tuple-element.51.grad_a_ref), channel_id=1, source_target_pairs={{0,1},{1,0},{2,3},{3,2},{4,5},{5,4},{6,7},{7,6},{8,9},{9,8},{10,11... | collective-permute-start | bytes 9437192 | tf_op jit(solution)/shard_map/ppermute | solution.py:499
  184.4 45.6 %collective-permute-start.7 = (bf16[2048,768]{1,0:T(8,128)(2,1)}, bf16[2048,768]{1,0:T(8,128)(2,1)}, u32[]{:S(2)}, u32[]{:S(2)}) collective-permute-start(bf16[2048,768]{1,0:T(8,128)(2,1)} %get-tuple-element.52.mlp_a_ref), channel_id=1, source_target_pairs={{0,1},{1,0},{2,3},{3,2},{4,5},{5,4},{6,7},{7,6},{8,9},{9,8},{10,11... | collective-permute-start | bytes 9437192 | tf_op jit(solution)/shard_map/ppermute | solution.py:499
  186.2 15.5 %collective-permute-start.19 = (bf16[2,2,96,768]{3,2,1,0:T(8,128)(2,1)S(1)}, bf16[2,2,96,768]{3,2,1,0:T(8,128)(2,1)}, u32[]{:S(2)}, u32[]{:S(2)}) collective-permute-start(bf16[2,2,96,768]{3,2,1,0:T(8,128)(2,1)S(1)} %fusion.2), channel_id=1, source_target_pairs={{0,8},{4,12},{8,0},{12,4},{16,24},{20,28},{24,16},{28,20},{1,9},{5... | collective-permute-start | bytes 1769480 | tf_op jit(solution)/shard_map/ppermute | solution.py:499
  188.4 16.7 %collective-permute-start.16 = (bf16[2,2,96,768]{3,2,0,1:T(8,128)(2,1)}, bf16[2,2,96,768]{3,2,0,1:T(8,128)(2,1)}, u32[]{:S(2)}, u32[]{:S(2)}) collective-permute-start(bf16[2,2,96,768]{3,2,0,1:T(8,128)(2,1)} %fusion), channel_id=1, source_target_pairs={{0,4},{4,0},{8,12},{12,8},{16,20},{20,16},{24,28},{28,24},{1,5},{5... | collective-permute-start | bytes 1769480 | tf_op jit(solution)/shard_map/ppermute | solution.py:499
  191.8 13.3 %copy-start.20 = (f32[768,768]{1,0:T(8,128)S(1)}, f32[768,768]{1,0:T(8,128)}, u32[]{:S(2)}) copy-start(f32[768,768]{1,0:T(8,128)} %get-tuple-element.76) | copy-start | bytes 7077892
  203.3 15.5 %collective-permute-start.20 = (bf16[2,96,768]{2,1,0:T(8,128)(2,1)S(1)}, bf16[2,96,768]{2,1,0:T(8,128)(2,1)S(1)}, u32[]{:S(2)}, u32[]{:S(2)}) collective-permute-start(bf16[2,96,768]{2,1,0:T(8,128)(2,1)S(1)} %fusion.5), channel_id=1, source_target_pairs={{0,16},{4,20},{8,24},{12,28},{16,0},{20,4},{24,8},{28,12},{1,17},{... | collective-permute-start | bytes 884744 | tf_op jit(solution)/shard_map/ppermute | solution.py:499
  206.4 14.7 %collective-permute-start.17 = (bf16[2,96,768]{2,1,0:T(8,128)(2,1)S(1)}, bf16[2,96,768]{2,1,0:T(8,128)(2,1)S(1)}, u32[]{:S(2)}, u32[]{:S(2)}) collective-permute-start(bf16[2,96,768]{2,1,0:T(8,128)(2,1)S(1)} %fusion.4), channel_id=1, source_target_pairs={{0,8},{4,12},{8,0},{12,4},{16,24},{20,28},{24,16},{28,20},{1,9},{5... | collective-permute-start | bytes 884744 | tf_op jit(solution)/shard_map/ppermute | solution.py:499
  218.9 11.1 %copy-start.7 = (bf16[384,768]{1,0:T(8,128)(2,1)S(1)}, bf16[384,768]{1,0:T(8,128)(2,1)}, u32[]{:S(2)}) copy-start(bf16[384,768]{1,0:T(8,128)(2,1)} %copy-done.5) | copy-start | bytes 1769476
  218.9 11.1 %copy-start.8 = (f32[1,768]{1,0:T(1,128)S(1)}, f32[1,768]{1,0:T(1,128)}, u32[]{:S(2)}) copy-start(f32[1,768]{1,0:T(1,128)} %reshape.135.gain_ref) | copy-start | bytes 9220
  219.0 5.7 %collective-permute-start.21 = (bf16[96,768]{1,0:T(8,128)(2,1)S(1)}, bf16[96,768]{1,0:T(8,128)(2,1)S(1)}, u32[]{:S(2)}, u32[]{:S(2)}) collective-permute-start(bf16[96,768]{1,0:T(8,128)(2,1)S(1)} %fusion.9), channel_id=1, source_target_pairs={{0,4},{4,0},{8,12},{12,8},{16,20},{20,16},{24,28},{28,24},{1,5},{5... | collective-permute-start | bytes 442376 | tf_op jit(solution)/shard_map/ppermute | solution.py:499
  221.2 8.0 %collective-permute-start.18 = (bf16[96,768]{1,0:T(8,128)(2,1)S(1)}, bf16[96,768]{1,0:T(8,128)(2,1)S(1)}, u32[]{:S(2)}, u32[]{:S(2)}) collective-permute-start(bf16[96,768]{1,0:T(8,128)(2,1)S(1)} %fusion.8), channel_id=1, source_target_pairs={{0,16},{4,20},{8,24},{12,28},{16,0},{20,4},{24,8},{28,12},{1,17},{... | collective-permute-start | bytes 442376 | tf_op jit(solution)/shard_map/ppermute | solution.py:499
  230.0 14.2 %copy-start.13 = (bf16[2048,384]{1,0:T(8,128)(2,1)S(1)}, bf16[2048,384]{1,0:T(8,128)(2,1)}, u32[]{:S(2)}) copy-start(bf16[2048,384]{1,0:T(8,128)(2,1)} %copy-done.12) | copy-start | bytes 4718596
  230.0 14.2 %copy-start.15 = (bf16[2048,384]{1,0:T(8,128)(2,1)S(1)}, bf16[2048,384]{1,0:T(8,128)(2,1)}, u32[]{:S(2)}) copy-start(bf16[2048,384]{1,0:T(8,128)(2,1)} %copy-done.14) | copy-start | bytes 4718596
  230.0 14.2 %copy-start.17 = (bf16[2048,384]{1,0:T(8,128)(2,1)S(1)}, bf16[2048,384]{1,0:T(8,128)(2,1)}, u32[]{:S(2)}) copy-start(bf16[2048,384]{1,0:T(8,128)(2,1)} %copy-done.16) | copy-start | bytes 4718596
  230.0 14.2 %copy-start.19 = (f32[16,8,256]{2,1,0:T(8,128)S(1)}, f32[16,8,256]{2,1,0:T(8,128)}, u32[]{:S(2)}) copy-start(f32[16,8,256]{2,1,0:T(8,128)} %copy-done.18) | copy-start | bytes 393220
  285.9 1.2 copy-start.11
  308.9 3.9 %collective-permute-start.9 = (f32[2,2,720]{2,1,0:T(2,128)S(1)}, f32[2,2,720]{2,1,0:T(2,128)S(1)}, u32[]{:S(2)}, u32[]{:S(2)}) collective-permute-start(f32[2,2,720]{2,1,0:T(2,128)S(1)} %bitcast.87), channel_id=1, source_target_pairs={{0,4},{4,0},{8,12},{12,8},{16,20},{20,16},{24,28},{28,24},{1,5},{5... | collective-permute-start | bytes 34568 | tf_op jit(solution)/shard_map/ppermute | solution.py:499
  311.1 40.9 %collective-permute-start.8 = (bf16[2048,768]{1,0:T(8,128)(2,1)}, bf16[2048,768]{1,0:T(8,128)(2,1)}, u32[]{:S(2)}, u32[]{:S(2)}) collective-permute-start(bf16[2048,768]{1,0:T(8,128)(2,1)} %get-tuple-element.61.grad_a_ref), channel_id=1, source_target_pairs={{0,1},{1,0},{2,3},{3,2},{4,5},{5,4},{6,7},{7,6},{8,9},{9,8},{10,11... | collective-permute-start | bytes 9437192 | tf_op jit(solution)/shard_map/ppermute | solution.py:499
  312.8 3.7 %collective-permute-start.10 = (f32[2,720]{1,0:T(2,128)S(1)}, f32[2,720]{1,0:T(2,128)S(1)}, u32[]{:S(2)}, u32[]{:S(2)}) collective-permute-start(f32[2,720]{1,0:T(2,128)S(1)} %bitcast.88), channel_id=1, source_target_pairs={{0,8},{4,12},{8,0},{12,4},{16,24},{20,28},{24,16},{28,20},{1,9},{5... | collective-permute-start | bytes 17288 | tf_op jit(solution)/shard_map/ppermute | solution.py:499
  313.0 14.8 %collective-permute-start.13 = (bf16[2,2,96,768]{3,2,1,0:T(8,128)(2,1)S(1)}, bf16[2,2,96,768]{3,2,1,0:T(8,128)(2,1)}, u32[]{:S(2)}, u32[]{:S(2)}) collective-permute-start(bf16[2,2,96,768]{3,2,1,0:T(8,128)(2,1)S(1)} %fusion.1), channel_id=1, source_target_pairs={{0,4},{4,0},{8,12},{12,8},{16,20},{20,16},{24,28},{28,24},{1,5},{5... | collective-permute-start | bytes 1769480 | tf_op jit(solution)/shard_map/ppermute | solution.py:499
  316.5 4.6 %collective-permute-start.11 = (f32[720]{0:T(1024)S(1)}, f32[720]{0:T(1024)S(1)}, u32[]{:S(2)}, u32[]{:S(2)}) collective-permute-start(f32[720]{0:T(1024)S(1)} %get-tuple-element.122), channel_id=1, source_target_pairs={{0,16},{4,20},{8,24},{12,28},{16,0},{20,4},{24,8},{28,12},{1,17},{... | collective-permute-start | bytes 8648 | tf_op jit(solution)/shard_map/ppermute | solution.py:499
  321.2 10.7 %collective-permute-start.12 = (f32[384]{0:T(512)S(1)}, f32[384]{0:T(512)S(1)}, u32[]{:S(2)}, u32[]{:S(2)}) collective-permute-start(f32[384]{0:T(512)S(1)} %slice.70), channel_id=1, source_target_pairs={{0,1},{1,0},{2,3},{3,2},{4,5},{5,4},{6,7},{7,6},{8,9},{9,8},{10,11... | collective-permute-start | bytes 4616 | tf_op jit(solution)/shard_map/ppermute | solution.py:499
  329.5 9.6 %collective-permute-start.14 = (bf16[2,96,768]{1,2,0:T(8,128)(2,1)S(1)}, bf16[2,96,768]{1,2,0:T(8,128)(2,1)S(1)}, u32[]{:S(2)}, u32[]{:S(2)}) collective-permute-start(bf16[2,96,768]{1,2,0:T(8,128)(2,1)S(1)} %fusion.3), channel_id=1, source_target_pairs={{0,8},{4,12},{8,0},{12,4},{16,24},{20,28},{24,16},{28,20},{1,9},{5... | collective-permute-start | bytes 884744 | tf_op jit(solution)/shard_map/ppermute | solution.py:499
  339.1 12.9 %copy-start.2 = (bf16[2048,768]{1,0:T(8,128)(2,1)S(1)}, bf16[2048,768]{1,0:T(8,128)(2,1)}, u32[]{:S(2)}) copy-start(bf16[2048,768]{1,0:T(8,128)(2,1)} %x_ref.7) | copy-start | bytes 9437188
  339.2 9.6 %collective-permute-start.15 = (bf16[96,768]{0,1:T(8,128)(2,1)S(1)}, bf16[96,768]{0,1:T(8,128)(2,1)S(1)}, u32[]{:S(2)}, u32[]{:S(2)}) collective-permute-start(bf16[96,768]{0,1:T(8,128)(2,1)S(1)} %fusion.7), channel_id=1, source_target_pairs={{0,16},{4,20},{8,24},{12,28},{16,0},{20,4},{24,8},{28,12},{1,17},{... | collective-permute-start | bytes 442376 | tf_op jit(solution)/shard_map/ppermute | solution.py:499
  352.0 2.8 copy-start
  354.8 1.9 copy-start.3
